TPU v7x, 512 devices: a whole 4x8x8 slice. The times are simulated.
512 devices in a mesh: ep: 16 (over y, core), tp: 32 (over z, x).
Axes of the slice: x: 4, y: 8, z: 8, core: 2. Of those that a mesh axis runs over, the one named last changes fastest.
Arguments:
- attn_out: bfloat16 [2048, 2048], P('ep'), may hold values from -6 to 6
- residual_in: bfloat16 [2048, 2048], P('ep'), may hold values from -6 to 6
- w_out: bfloat16 [2048, 2048], P(None, 'tp'), may hold values from -0.125 to 0.125
- gain_in: float32 [2048], replicated, may hold values from 0.1 to 1.9
- router_logits: float32 [2048, 8], P('ep'), may hold values from -8 to 8
- expert_ids: int32 [2048, 2], P('ep'), may hold values from 0 to 7, all different within a row; in each aligned block of 128 rows (0 to 127, 128 to 255, ...) at most 64 rows name the same one
- copy_of: int32 [16, 8], replicated, may hold values from 0 to 15, as said below
- w_gate: bfloat16 [16, 2048, 5632], P('ep', None, 'tp')
- w_up: bfloat16 [16, 2048, 5632], P('ep', None, 'tp')
- w_down: bfloat16 [16, 5632, 2048], P('ep', 'tp')
- gain_out: float32 [2048], replicated, may hold values from 0.1 to 1.9
Outputs:
- layer_out: bfloat16 [2048, 2048], P(('ep', 'tp'))
- next_input: bfloat16 [2048, 2048], P(('ep', 'tp'))
Inputs may be any that keep to these rules, and one draw needn't show every extreme that they name: `expert_ids`: each row names 2 different experts. Within the rows of one ep group (aligned blocks of 128 rows) no expert is named by more than 64 rows, and in every draw some group has an expert named by exactly 64 rows. copy_of[s, e] is a copy of expert e, so different experts of one group go to different copies; copies of one expert carry equal weights.
All inputs are finite; a program needn't handle non-finite values.
Results may differ from a plain program's by a relative error of at most 0.019.
Values may be sent and summed in bfloat16 or wider, within the bound.
A program may use at most 64 MiB of HBM per device.

v0:
```python
import jax
import jax.numpy as jnp
from jax import lax
from jax.sharding import PartitionSpec as P


def rms_scale(values, gain):
    mean_square = jnp.mean(values * values, axis=-1, keepdims=True)
    return values * lax.rsqrt(mean_square + 1e-06) * gain


def expert_terms(slots, gate_weight, up_weight, down_weight):
    gate_value = jnp.einsum(
        "scmd,cdf->scmf", slots, gate_weight, preferred_element_type=jnp.float32
    )
    up_value = jnp.einsum("scmd,cdf->scmf", slots, up_weight, preferred_element_type=jnp.float32)
    hidden = (jax.nn.silu(gate_value) * up_value).astype(jnp.bfloat16)
    return jnp.einsum("scmf,cfd->scmd", hidden, down_weight, preferred_element_type=jnp.float32)


def per_device(
    attn_out,
    residual_in,
    w_out,
    gain_in,
    router_logits,
    expert_ids,
    copy_of,
    w_gate,
    w_up,
    w_down,
    gain_out,
):
    group_rows = attn_out.shape[0]
    model_width = attn_out.shape[1]
    tp_count = lax.axis_size("tp")
    ep_count = lax.axis_size("ep")
    own_rows = group_rows // tp_count
    capacity = group_rows // 2
    copies_here = w_gate.shape[0]
    copies_all = copies_here * ep_count
    experts_all = router_logits.shape[1]
    group_index = lax.axis_index("ep")
    tp_index = lax.axis_index("tp")
    columns = jnp.dot(attn_out, w_out, preferred_element_type=jnp.float32).astype(jnp.bfloat16)
    projected = lax.all_gather(columns, "tp", axis=1, tiled=True)
    carried = (residual_in.astype(jnp.float32) + projected.astype(jnp.float32)).astype(jnp.bfloat16)
    normed = rms_scale(carried.astype(jnp.float32), gain_in).astype(jnp.bfloat16)
    expert_grid = jnp.arange(experts_all, dtype=jnp.int32)
    picked = expert_ids[:, :, None] == expert_grid[None, None, :]
    chosen = jnp.sum(jnp.where(picked, router_logits[:, None, :], 0.0), axis=2)
    gate_share = jax.nn.sigmoid(chosen - chosen[:, ::-1])
    group_copies = lax.dynamic_slice_in_dim(copy_of, group_index, 1, 0)[0]
    target = jnp.sum(jnp.where(picked, group_copies[None, None, :], 0), axis=2)
    copy_hits = (
        target[:, :, None] == jnp.arange(copies_all, dtype=jnp.int32)[None, None, :]
    ).astype(jnp.int32)
    per_row = jnp.sum(copy_hits, axis=1)
    before = jnp.cumsum(per_row, axis=0) - per_row
    position = jnp.sum(copy_hits * before[:, None, :], axis=2)
    slot_index = target * capacity + position
    row_numbers = jnp.broadcast_to(
        jnp.arange(group_rows, dtype=jnp.int32)[:, None], slot_index.shape
    )
    slot_rows = (
        jnp.zeros((copies_all * capacity,), jnp.int32)
        .at[slot_index.reshape(-1)]
        .set(row_numbers.reshape(-1))
    )
    rows_table = slot_rows.reshape(ep_count, copies_here, capacity)
    outgoing = jnp.take(normed, rows_table, axis=0)
    arrived = lax.all_to_all(outgoing, "ep", split_axis=0, concat_axis=0, tiled=True)
    partial_value = expert_terms(arrived, w_gate, w_up, w_down)
    summed = lax.psum_scatter(
        partial_value.astype(jnp.bfloat16), "tp", scatter_dimension=2, tiled=True
    )
    returned = lax.all_to_all(summed, "ep", split_axis=0, concat_axis=0, tiled=True)
    own_target = lax.dynamic_slice_in_dim(target, tp_index * own_rows, own_rows, 0)
    own_position = lax.dynamic_slice_in_dim(position, tp_index * own_rows, own_rows, 0)
    own_gates = lax.dynamic_slice_in_dim(gate_share, tp_index * own_rows, own_rows, 0)
    portion = lax.all_gather(returned, "tp", axis=2, tiled=True)
    span_rows = portion.shape[2]
    flat_portion = portion.reshape(copies_all, span_rows, model_width)
    inside = (own_position >= 0) & (own_position < span_rows)
    picked_rows = flat_portion[own_target, jnp.clip(own_position, 0, span_rows - 1)]
    row_weights = jnp.where(inside, own_gates, 0.0)
    mixture = jnp.sum(row_weights[:, :, None] * picked_rows.astype(jnp.float32), axis=1)
    own_carried = lax.dynamic_slice_in_dim(carried, tp_index * own_rows, own_rows, 0)
    layer_out = (own_carried.astype(jnp.float32) + mixture).astype(jnp.bfloat16)
    next_input = rms_scale(layer_out.astype(jnp.float32), gain_out).astype(jnp.bfloat16)
    return (layer_out, next_input)


def solution(mesh):
    return jax.shard_map(
        per_device,
        mesh=mesh,
        in_specs=(
            P("ep", None),
            P("ep", None),
            P(None, "tp"),
            P(),
            P("ep", None),
            P("ep", None),
            P(),
            P("ep", None, "tp"),
            P("ep", None, "tp"),
            P("ep", "tp", None),
            P(),
        ),
        out_specs=(P(("ep", "tp"), None), P(("ep", "tp"), None)),
        check_vma=False,
    )
```

profile of v0, /device:TPU:8, one launch (start us, length us, event | category | flops | bytes accessed | tf_op | source)
XLA Modules:
  0.0 536.4 jit_solution(7059032426642041962)
XLA Ops:
  7.2 0.0 copy-start
  7.2 0.0 copy-start.3
  7.2 0.0 reduce-scatter.2.cloned.1.call-start
  7.2 0.9 dynamic-slice_reduce_fusion
  8.2 0.8 select_reduce_fusion.2
  8.9 0.1 copy.68
  9.0 0.2 reduce_window_sum.11
  9.2 0.1 copy.70
  9.3 0.1 copy.72
  9.4 0.1 add.110
  9.6 0.1 reshape.207
  9.8 1.4 scatter_custom_fusion
  11.2 0.1 reshape.182
  11.2 0.1 reshape.181
  11.3 0.1 reshape.191
  11.4 1.4 convolution_convert_fusion
  12.8 55.7 %all_gather.6 = bf16[128,2048]{0,1:T(8,128)(2,1)S(1)} all-gather(bf16[128,64]{0,1:T(8,128)(2,1)S(1)} %convolution_convert_fusion), channel_id=1, replica_groups=mesh['ep'=16,'tp'=32] {'tp'}, dimensions={1}, use_global_device_ids=true | all-gather | bytes 540672 | tf_op jit(solution)/shard_map/all_gather | solution.py:46
  68.5 0.2 copy.67
  68.7 1.3 fusion.19
  70.0 0.0 copy-done.3
  70.0 0.2 fusion.21
  70.2 6.0 %gather_fusion = bf16[1024,2048]{1,0:T(8,128)(2,1)} fusion(bf16[128,2048]{1,0:T(8,128)(2,1)S(1)} %fusion.21, s32[1024]{0:T(1024)S(1)} %broadcast_clamp_fusion), kind=kCustom, calls=%fused_computation | custom fusion | bytes 8392704 | tf_op jit(solution)/shard_map/jit(_take)/gather | solution.py:71
  76.3 2.6 broadcast_select_fusion
  78.9 0.0 copy-start.7
  78.9 100.5 %all_to_all.10 = bf16[16,1,64,2048]{3,2,1,0:T(8,128)(2,1)S(1)} all-to-all(bf16[16,1,64,2048]{3,2,1,0:T(8,128)(2,1)S(1)} %broadcast_select_fusion), channel_id=1, replica_groups=mesh['ep'=16,'tp'=32] {'ep'}, dimensions={0} | all-to-all | bytes 8388608 | tf_op jit(solution)/shard_map/all_to_all | solution.py:72
  179.4 0.0 copy-start.1
  179.4 2.0 copy-done.1
  181.4 0.0 copy-done.7
  181.4 0.0 copy-start.8
  181.4 2.3 fusion.4
  183.7 0.0 copy-done
  183.7 0.0 copy-done.8
  183.7 8.8 %convert_bitcast_fusion = bf16[16,1,64,2048]{3,2,0,1:T(8,128)(2,1)} fusion(bf16[16,1,64,2048]{3,2,1,0:T(8,128)(2,1)} %copy-done.1, f32[16,1,64,176]{3,2,0,1:T(8,128)} %fusion.4, bf16[1,176,2048]{2,1,0:T(8,128)(2,1)S(1)} %copy-done, bf16[1,2048,176]{1,2,0:T(8,128)(2,1)S(1)} %copy-done.8), kind=kOutput, calls=%fused_computation.8 | convolution fusion | flops 1479573504 | bytes 10551296 | tf_op jit(solution)/shard_map/scmf,cfd->scmd/dot_general | solution.py:18
  192.5 6.5 %copy.74 = bf16[16,1,64,2048]{3,0,1,2:T(8,128)(2,1)} copy(bf16[16,1,64,2048]{3,2,0,1:T(8,128)(2,1)} %convert_bitcast_fusion) | data formatting | bytes 8388608 | tf_op jit(solution)/shard_map/convert_element_type | solution.py:75
  198.9 0.0 copy-start.5
  198.9 0.0 copy-start.6
  198.9 0.0 reduce-scatter.2.cloned.1.call-update
  199.0 0.0 all-gather.2.cloned.1.call-start
  199.0 221.9 %reduce-scatter.2.cloned.1.call-done = bf16[16,1,2,2048]{3,0,1,2:T(8,128)(2,1)} async-done(((bf16[16,1,64,2048]{3,0,1,2:T(8,128)(2,1)}), bf16[16,1,2,2048]{3,0,1,2:T(8,128)(2,1)}) %reduce-scatter.2.cloned.1.call-update) | async-done | bytes 131088 | tf_op jit(solution)/shard_map/reduce_scatter | solution.py:74
  420.9 1.0 copy.75
  422.0 14.5 %all_to_all.11 = bf16[16,1,2,2048]{3,2,1,0:T(2,128)(2,1)S(1)} all-to-all(bf16[16,1,2,2048]{3,2,1,0:T(2,128)(2,1)S(1)} %copy.75), channel_id=1, replica_groups=mesh['ep'=16,'tp'=32] {'ep'}, dimensions={0} | all-to-all | bytes 262144 | tf_op jit(solution)/shard_map/all_to_all | solution.py:77
  436.5 0.7 copy.76
  437.2 0.0 all-gather.2.cloned.1.call-update
  437.2 0.1 fusion.37
  437.3 0.1 copy.78
  437.4 0.1 reshape.197
  437.5 0.0 copy-done.5
  437.5 0.0 copy-done.6
  437.6 0.1 and_select_fusion
  437.6 0.1 copy.71
  437.7 0.0 copy-start.4
  437.7 82.9 %all-gather.2.cloned.1.call-done = bf16[16,1,64,2048]{3,0,1,2:T(8,128)(2,1)} async-done(((bf16[16,1,2,2048]{3,0,1,2:T(8,128)(2,1)}), bf16[16,1,64,2048]{3,0,1,2:T(8,128)(2,1)}) %all-gather.2.cloned.1.call-update) | async-done | bytes 4194320 | tf_op jit(solution)/shard_map/all_gather | solution.py:81
  520.6 6.5 %copy.80 = bf16[16,1,64,2048]{3,2,0,1:T(8,128)(2,1)} copy(bf16[16,1,64,2048]{3,0,1,2:T(8,128)(2,1)} %all-gather.2.cloned.1.call-done) | data formatting | bytes 8388608 | tf_op jit(solution)/shard_map/all_gather | solution.py:81
  527.0 1.4 gather_fusion.1
  528.5 0.2 multiply_reduce_fusion
  528.7 0.1 fusion.29
  528.8 0.0 copy-start.2
  528.8 0.0 copy-done.4
  528.8 0.7 fusion.31
  529.5 0.0 copy-done.2
  (15 shorter events, 0.2 us)
Async XLA Ops:
  7.2 176.5 %copy-start = (bf16[1,176,2048]{2,1,0:T(8,128)(2,1)S(1)}, bf16[1,176,2048]{2,1,0:T(8,128)(2,1)}, u32[]{:S(2)}) copy-start(bf16[1,176,2048]{2,1,0:T(8,128)(2,1)} %param.20) | copy-start | bytes 2162692
  7.2 62.8 %copy-start.3 = (f32[2048]{0:T(1024)S(1)}, f32[2048]{0:T(1024)}, u32[]{:S(2)}) copy-start(f32[2048]{0:T(1024)} %param.14) | copy-start | bytes 24580
  7.2 413.7 %reduce-scatter.2.cloned.1.call-start = ((), (), s32[]{:S(2)}) async-start(), calls=%async_computation.3 | async-start | bytes 4325376 | tf_op jit(solution)/shard_map/reduce_scatter | solution.py:74
  78.9 102.5 %copy-start.7 = (bf16[1,2048,176]{1,2,0:T(8,128)(2,1)S(1)}, bf16[1,2048,176]{1,2,0:T(8,128)(2,1)}, u32[]{:S(2)}) copy-start(bf16[1,2048,176]{1,2,0:T(8,128)(2,1)} %param.18) | copy-start | bytes 2162692
  179.4 2.0 copy-start.1
  181.4 2.3 copy-start.8
  198.9 238.6 %copy-start.5 = (f32[128,8]{0,1:T(8,128)S(1)}, f32[128,8]{0,1:T(8,128)}, u32[]{:S(2)}) copy-start(f32[128,8]{0,1:T(8,128)} %param.15) | copy-start | bytes 12292
  198.9 238.6 %copy-start.6 = (s32[128,2]{0,1:T(2,128)S(1)}, s32[128,2]{0,1:T(2,128)}, u32[]{:S(2)}) copy-start(s32[128,2]{0,1:T(2,128)} %param.16) | copy-start | bytes 3076
  199.0 321.6 %all-gather.2.cloned.1.call-start = ((), (), s32[]{:S(2)}) async-start(), calls=%async_computation.4 | async-start | bytes 4325376 | tf_op jit(solution)/shard_map/all_gather | solution.py:81
  437.7 91.1 %copy-start.4 = (f32[2048]{0:T(1024)S(1)}, f32[2048]{0:T(1024)}, u32[]{:S(2)}) copy-start(f32[2048]{0:T(1024)} %param.21) | copy-start | bytes 24580
  528.8 0.7 copy-start.2
Sparse Core Ops, SparseCore 0:
  199.1 221.8 reduce-scatter.1
  437.3 83.1 all-gather.1
where the time goes:
time: 537 us; the launch traced here: 536 us
  waiting for transfers between devices  305 us (57%)
  blocking collectives  171 us (32%)
  local copies, waits for them, and re-layouts  27.7 us (5%)
  between operations  14.2 us (3%)
  matrix products  12.5 us (2%)
  other arithmetic  6.33 us (1%)
    reduce_scatter x1, waiting for transfers between devices, per_device(): lax.psum_scatter(partial_value.astype(jnp.bfloat16), 'tp', scatter_dimens...  222 us
    all_to_all x1, blocking collectives, per_device(): lax.all_to_all(outgoing, 'ep', split_axis=0, concat_axis=0, tiled=True)  100 us
    all_gather x1, waiting for transfers between devices, per_device(): portion = lax.all_gather(returned, 'tp', axis=2, tiled=True)  82.9 us
    all_gather x1, blocking collectives, per_device(): projected = lax.all_gather(columns, 'tp', axis=1, tiled=True)  55.7 us
    all_to_all x1, blocking collectives, per_device(): lax.all_to_all(summed, 'ep', split_axis=0, concat_axis=0, tiled=True)  14.5 us
  transfers between devices with their start and end apart: 2, of which 2 were waited for; matrix products, arithmetic and copies ran while one was open for 0% of the time, Pallas kernels for 0%

commit v1 on v0

v1 whole, which is shorter than its diff:
```python
import functools
import heapq

import jax
import jax.numpy as jnp
from jax import lax
from jax.experimental import pallas as pl
from jax.experimental.pallas import tpu as pltpu
from jax.sharding import PartitionSpec as P

MESH = pl.DeviceIdType.MESH
F32 = jnp.float32
BF16 = jnp.bfloat16
NX = 4
COLS = 64
GROUP = 128
CAP = 64
SIGNS = (1, -1)


def row_range(parts, part, sign, dist, count):
    start, size = parts[part]
    if 2 * dist == count:
        half = size // 2
        return (start, half) if sign > 0 else (start + half, half)
    return (start, size)


def ordered(sends, ready):
    rate, latency = 46500.0, 1.7
    heap, serial = [], 0
    for when, event in ready:
        heapq.heappush(heap, (when, serial, event))
        serial += 1
    done, free, waiting, ops = set(), {}, dict(sends), []

    def release(now):
        nonlocal serial
        for key in [k for k, v in waiting.items() if v[2] <= done]:
            link, size, _ = waiting.pop(key)
            begin = max(now, free.get(link, 0.0))
            free[link] = begin + size / rate
            ops.append(("start", key))
            heapq.heappush(heap, (free[link] + latency, serial, ("wait", key)))
            serial += 1

    release(0.0)
    while heap:
        now, _, event = heapq.heappop(heap)
        ops.append(event)
        done.add(event)
        release(now)
    assert not waiting
    return ops


def gather_plan(nz, nx, parts):
    count = {"z": nz, "x": nx}
    sends = {}
    for part, (first, second) in (("a", ("x", "z")), ("b", ("z", "x"))):
        for axis in (first, second):
            n = count[axis]
            for other in range(1 if axis == first else count[first]):
                for dist in range(1, n // 2 + 1):
                    for sign in SIGNS:
                        need = set()
                        if dist > 1:
                            need.add(("wait", (part, axis, sign, dist - 1, other)))
                        elif axis == second and other:
                            m = count[first]
                            if 2 * other <= m:
                                need.add(("wait", (part, first, 1, other, 0)))
                            if 2 * other >= m:
                                need.add(("wait", (part, first, -1, m - other, 0)))
                        size = row_range(parts, part, sign, dist, n)[1] * 256
                        sends[(part, axis, sign, dist, other)] = ((axis, sign), size, need)
    return list(sends), ordered(sends, [])


def reduce_plan(nz, nx, parts, step):
    count = {"z": nz, "x": nx}
    far = sorted(range(nz), key=lambda d: (-min(d, nz - d), d))
    chunk_at = [((i + 1) * step, ("chunk", dz)) for i, dz in enumerate(far)]
    sends = {}
    for part, (first, second) in (("a", ("z", "x")), ("b", ("x", "z"))):
        for axis in (first, second):
            n = count[axis]
            for other in range(count[second] if axis == first else 1):
                for dist in range(n // 2, 0, -1):
                    for sign in SIGNS:
                        offset = (sign * dist) % n
                        dz = offset if axis == "z" else other
                        need = {("chunk", dz)}
                        if 2 * dist < n:
                            need.add(("wait", (part, axis, sign, dist + 1, other)))
                        if axis == second:
                            for s in SIGNS:
                                need.add(("wait", (part, first, s, 1, offset)))
                        size = row_range(parts, part, sign, dist, n)[1] * 256
                        sends[(part, axis, sign, dist, other)] = ((axis, sign), size, need)
    return list(sends), ordered(sends, chunk_at), far


def iota(shape, dim):
    return lax.broadcasted_iota(jnp.int32, shape, dim)


def left_half(shape):
    return iota(shape, len(shape) - 1) < COLS


def swap(value):
    return pltpu.roll(value, COLS, value.ndim - 1)


def rank_before(hits):
    tri = (iota((GROUP, GROUP), 0) < iota((GROUP, GROUP), 1)).astype(F32).astype(BF16)
    return jnp.dot(hits.astype(BF16), tri, preferred_element_type=F32)


def targets_of(ids, copies):
    experts = copies.shape[1]
    total = jnp.zeros(ids.shape, F32)
    for e in range(experts):
        total = total + jnp.where(ids == float(e), copies[:, e : e + 1], 0.0)
    return total


def collect_kernel(nep, nt, attn, w_out, residual, ids, copies, rows_out, load_out, send_sem, recv_sem):
    ep, tp = lax.axis_index("ep"), lax.axis_index("tp")
    ny = nep // 2
    y, core = ep // 2, lax.rem(ep, 2)
    mate = 2 * y + (1 - core)

    def peer(k):
        return 2 * lax.rem(y + k, ny) + core

    barrier = pltpu.get_barrier_semaphore()
    for k in range(1, ny):
        pl.semaphore_signal(barrier, inc=1, device_id={"ep": peer(k), "tp": tp}, device_id_type=MESH)
    pl.semaphore_signal(barrier, inc=1, device_id={"ep": mate, "tp": tp}, device_id_type=MESH)

    product = jnp.dot(attn[...], w_out[...], preferred_element_type=F32).astype(BF16).astype(F32)
    pair = residual[:, pl.ds(pl.multiple_of((tp // 2) * 128, 128), 128)].astype(F32)
    left = left_half((GROUP, 128))
    odd = lax.rem(tp, 2) == 1
    pair = jnp.where(odd, swap(pair), pair)
    carried = pair + jnp.concatenate([product, product], axis=1)
    packed = jnp.where(left[:CAP], carried[:CAP], swap(carried[CAP:]))
    rows_out[ep, 0:CAP, :] = packed.astype(BF16)
    names = ids[...].astype(F32)
    rows_out[ep, CAP : CAP + 16, :] = jnp.concatenate(
        [names, jnp.zeros((14, GROUP), F32)], axis=0
    ).astype(BF16)

    pl.semaphore_wait(barrier, ny)

    def copy(slot, where, index):
        return pltpu.make_async_remote_copy(
            src_ref=rows_out.at[slot],
            dst_ref=rows_out.at[slot],
            send_sem=send_sem.at[index],
            recv_sem=recv_sem.at[index],
            device_id={"ep": where, "tp": tp},
            device_id_type=MESH,
        )

    order = sorted(range(1, ny), key=lambda k: (-min(k, ny - k), k))
    own = [copy(ep, mate, 0)] + [copy(ep, peer(k), k) for k in order]
    for c in own:
        c.start()
    passed = []
    for k in reversed(order):
        came = 2 * lax.rem(y + ny - k, ny) + core
        copy(came, peer(k), k).wait_recv()
        relay = copy(came, mate, ny + k)
        relay.start()
        passed.append(relay)
    copy(2 * y + 1 - core, mate, 0).wait_recv()
    for k in reversed(order):
        copy(2 * lax.rem(y + ny - k, ny) + 1 - core, mate, ny + k).wait_recv()
    for c in own + passed:
        c.wait_send()

    table = rows_out[:, CAP : CAP + 16, :].astype(F32)
    first = targets_of(table[:, 0, :], copies[...])
    second = targets_of(table[:, 1, :], copies[...])
    most = jnp.zeros((1, 1), F32)
    for q in range(ny):
        lo, hi = float(2 * q), float(2 * q + 1)
        hits = ((first >= lo) & (first <= hi)).astype(F32) + ((second >= lo) & (second <= hi)).astype(F32)
        most = jnp.maximum(most, jnp.sum(jnp.sum(hits, axis=1, keepdims=True), axis=0, keepdims=True))
    load_out[...] = jnp.broadcast_to(most, (8, 128)).astype(jnp.int32)


def expert_kernel(
    nep, nt, width, half_rows,
    rows, copies, logits, gain_in, gain_out, w_gate, w_up, w_down,
    layer_out, next_out,
    pick, flat_l, flat_r, got, full, gates, ups, downs, hid, share, landed, fin, ret_pick, ret_l, ret_r,
    back, slots, outgoing, incoming, whole,
    gs_send, gs_recv, rs_send, rs_recv, w_local, w_send, w_recv, x_send, x_recv, e_send, e_recv, f_send, f_recv,
):
    ep, tp = lax.axis_index("ep"), lax.axis_index("tp")
    nx = NX if nt > 8 else 2
    nz = nt // nx
    ny = nep // 2
    y, core = ep // 2, lax.rem(ep, 2)
    mate = 2 * y + (1 - core)
    z, x = tp // nx, lax.rem(tp, nx)
    hp = half_rows // 2
    a = (hp * 2 // 5) // 32 * 32
    parts = {"a": (0, a), "b": (a, hp - a)}
    own_rows = GROUP // nt

    def device(where_ep, where_tp):
        return {"ep": where_ep, "tp": where_tp}

    barrier = pltpu.get_barrier_semaphore()
    for k in range(1, nt):
        pl.semaphore_signal(
            barrier, inc=1, device_id=device(ep, lax.rem(tp + k, nt)), device_id_type=MESH
        )
    for k in range(1, nep):
        pl.semaphore_signal(
            barrier, inc=1, device_id=device(lax.rem(ep + k, nep), tp), device_id_type=MESH
        )

    own_weights = [
        pltpu.make_async_copy(src.at[0], dst.at[0], w_local.at[i])
        for i, (src, dst) in enumerate(((w_gate, gates), (w_up, ups), (w_down, downs)))
    ]
    for c in own_weights:
        c.start()

    table = rows[:, CAP : CAP + 16, :].astype(F32)
    aims = [targets_of(table[:, k, :], copies[...]) for k in range(2)]
    low = (2 * y).astype(F32)
    hits = [
        ((aims[0] == low + c).astype(F32) + (aims[1] == low + c).astype(F32)) for c in (0.0, 1.0)
    ]
    before = [rank_before(h) for h in hits]
    totals = [jnp.sum(h, axis=1, keepdims=True) for h in hits]
    lower = (iota((nep, nep), 1) < iota((nep, nep), 0)).astype(F32).astype(BF16)
    offsets = [
        jnp.dot(lower, jnp.broadcast_to(t, (nep, 128)).astype(BF16), preferred_element_type=F32)
        for t in totals
    ]
    count_low = jnp.sum(totals[0], axis=0, keepdims=True)
    starts = [offsets[0], offsets[1] + count_low]
    places = [starts[c] + before[c] for c in range(2)]
    spots = [
        jnp.where(
            aims[k] == low, places[0], jnp.where(aims[k] == low + 1.0, places[1], -1.0)
        )
        for k in range(2)
    ]

    left64 = left_half((CAP, 128))
    for s in range(nep):
        packed = rows[s, 0:CAP, :].astype(F32)
        other = swap(packed)
        at = s * GROUP
        flat_l[at : at + CAP, :] = jnp.where(left64, packed, 0.0).astype(BF16)
        flat_l[at + CAP : at + GROUP, :] = jnp.where(left64, other, 0.0).astype(BF16)
        flat_r[at : at + CAP, :] = jnp.where(left64, 0.0, other).astype(BF16)
        flat_r[at + CAP : at + GROUP, :] = jnp.where(left64, 0.0, packed).astype(BF16)
    base = (core * half_rows).astype(F32)
    piece = jnp.zeros((hp, 128), F32)
    for q, flat in enumerate((flat_l, flat_r)):
        line = iota((hp, 128), 0).astype(F32) + base + float(q * hp)
        for s in range(nep):
            hit = (spots[0][s : s + 1, :] == line) | (spots[1][s : s + 1, :] == line)
            pick[:, s * GROUP : (s + 1) * GROUP] = jnp.where(hit, 1.0, 0.0).astype(BF16)
        piece = piece + jnp.dot(pick[...], flat[...], preferred_element_type=F32)
    got[0, 0, :, :] = piece.astype(BF16)

    pl.semaphore_wait(barrier, nt - 1 + nep - 1)

    def move(src, dst, send, recv, where):
        return pltpu.make_async_remote_copy(
            src_ref=src, dst_ref=dst, send_sem=send, recv_sem=recv, device_id=where, device_id_type=MESH
        )

    mate_weights = [
        move(src.at[0], dst.at[1], w_send.at[i], w_recv.at[i], device(mate, tp))
        for i, (src, dst) in enumerate(((w_gate, gates), (w_up, ups), (w_down, downs)))
    ]

    def neighbour(axis, sign):
        if axis == "z":
            return device(ep, lax.rem(z + sign + nz, nz) * nx + x)
        return device(ep, z * nx + lax.rem(x + sign + nx, nx))

    count = {"z": nz, "x": nx}

    def slot_of(axis, offset, other):
        return (offset % nz, other) if axis == "z" else (other, offset % nx)

    keys, ops = gather_plan(nz, nx, parts)

    def gather_copy(key):
        part, axis, sign, dist, other = key
        start, size = row_range(parts, part, sign, dist, count[axis])
        src = slot_of(axis, sign * (dist - 1), other)
        dst = slot_of(axis, sign * dist, other)
        i = keys.index(key)
        return move(
            got.at[src[0], src[1], pl.ds(start, size), :],
            got.at[dst[0], dst[1], pl.ds(start, size), :],
            gs_send.at[i], gs_recv.at[i], neighbour(axis, sign),
        )

    sent = []
    for c in mate_weights:
        c.start()
        sent.append(c)
    for kind, key in ops:
        c = gather_copy(key)
        if kind == "start":
            c.start()
            sent.append(c)
        else:
            c.wait_recv()

    left = left_half((hp, 128))

    def join(i, carry):
        t0, t1 = 2 * i, 2 * i + 1
        p0, p1 = [
            got[lax.rem(z - t // nx + nz, nz), lax.rem(x - lax.rem(t, nx) + nx, nx)].astype(F32)
            for t in (t0, t1)
        ]
        lanes = pl.ds(pl.multiple_of(i * 128, 128), 128)
        full[0:hp, lanes] = jnp.where(left, p0, swap(p1)).astype(BF16)
        full[hp : 2 * hp, lanes] = jnp.where(left, swap(p0), p1).astype(BF16)
        return carry

    lax.fori_loop(0, nt // 2, join, 0)
    for c in own_weights:
        c.wait()
    for c in mate_weights:
        c.wait_recv()

    tile = 128
    count_own = jnp.broadcast_to(count_low, (tile, 1))
    core_f = core.astype(F32)

    def experts(i, carry):
        at = pl.ds(pl.multiple_of(i * tile, tile), tile)
        value = full[at, :].astype(F32)
        scale = lax.rsqrt(jnp.sum(value * value, axis=1, keepdims=True) * (1.0 / width) + 1e-06)
        normed = (value * scale * gain_in[...]).astype(BF16)
        spot = iota((tile, 1), 0).astype(F32) + base + (i * tile).astype(F32)
        in_low = (spot < count_own).astype(F32)
        mine = in_low * (1.0 - core_f) + (1.0 - in_low) * core_f
        for w, keep in ((0, mine), (1, 1.0 - mine)):
            gate = jnp.dot(normed, gates[w], preferred_element_type=F32)
            up = jnp.dot(normed, ups[w], preferred_element_type=F32)
            value_h = gate / (1.0 + jnp.exp(-gate)) * up
            hid[w, at, :] = jnp.where(keep > 0.5, value_h, 0.0).astype(BF16)
        return carry

    lax.fori_loop(0, half_rows // tile, experts, 0)

    rs_keys, rs_ops, far = reduce_plan(nz, nx, parts, 0.4)
    land_at, total = {}, 0
    for key in rs_keys:
        size = row_range(parts, key[0], key[2], key[3], count[key[1]])[1]
        land_at[key] = (total, size)
        total += size

    def reduce_copy(key):
        part, axis, sign, dist, other = key
        start, size = row_range(parts, part, sign, dist, count[axis])
        src = slot_of(axis, sign * dist, other)
        i = rs_keys.index(key)
        return move(
            share.at[src[0], src[1], pl.ds(start, size), :],
            landed.at[pl.ds(land_at[key][0], size), :],
            rs_send.at[i], rs_recv.at[i], neighbour(axis, sign),
        )

    def chunk(dz):
        zt = lax.rem(z + dz, nz)
        lanes = pl.ds(pl.multiple_of(zt * (nx * COLS), 128), nx * COLS)
        wd = [downs[w, :, lanes] for w in range(2)]
        sides = []
        for q in range(2):
            at = slice(q * hp, (q + 1) * hp)
            sides.append(
                jnp.dot(hid[0, at, :], wd[0], preferred_element_type=F32)
                + jnp.dot(hid[1, at, :], wd[1], preferred_element_type=F32)
            )
        for i in range(nx // 2):
            top, low_side = [v[:, i * 128 : (i + 1) * 128] for v in sides]
            d0 = lax.rem(2 * i - x + nx, nx)
            d1 = lax.rem(2 * i + 1 - x + nx, nx)
            share[dz, d0] = jnp.where(left, top, swap(low_side)).astype(BF16)
            share[dz, d1] = jnp.where(left, swap(top), low_side).astype(BF16)

    for kind, key in rs_ops:
        if kind == "chunk":
            chunk(key)
            continue
        c = reduce_copy(key)
        if kind == "start":
            c.start()
            sent.append(c)
        else:
            c.wait_recv()
            part, axis, sign, dist, other = key
            start, size = row_range(parts, part, sign, dist, count[axis])
            at = slot_of(axis, sign * (dist - 1), other)
            here = pl.ds(start, size)
            there = pl.ds(land_at[key][0], size)
            share[at[0], at[1], here, :] = (
                share[at[0], at[1], here, :].astype(F32) + landed[there, :].astype(F32)
            ).astype(BF16)

    swap_copy = move(share.at[0, 0], fin, x_send.at[0], x_recv.at[0], device(mate, tp))
    swap_copy.start()
    sent.append(swap_copy)
    start_own = jnp.where(core == 0, starts[0], starts[1])
    joint = 2 * half_rows
    lead = (iota((CAP // 2, joint), 1) - iota((CAP // 2, joint), 0)).astype(F32)
    for q in range(2):
        for s in range(nep):
            first_spot = start_own[s : s + 1, 0:1] + float(q * (CAP // 2))
            at = s * (CAP // 2)
            ret_pick[q, at : at + CAP // 2, :] = jnp.where(lead == first_spot, 1.0, 0.0).astype(BF16)
    swap_copy.wait_recv()
    here_v = share[0, 0].astype(F32)
    there_v = fin[...].astype(F32)
    zero_core = core == 0
    for h in range(2):
        v = jnp.where(zero_core, here_v, there_v) if h == 0 else jnp.where(zero_core, there_v, here_v)
        w = swap(v)
        at = h * half_rows
        ret_l[at : at + hp, :] = jnp.where(left, v, 0.0).astype(BF16)
        ret_l[at + hp : at + 2 * hp, :] = jnp.where(left, w, 0.0).astype(BF16)
        ret_r[at : at + hp, :] = jnp.where(left, 0.0, w).astype(BF16)
        ret_r[at + hp : at + 2 * hp, :] = jnp.where(left, 0.0, v).astype(BF16)
    blocks = jnp.dot(ret_pick[0], ret_l[...], preferred_element_type=F32)
    blocks = blocks + jnp.dot(ret_pick[1], ret_r[...], preferred_element_type=F32)
    back[...] = blocks.astype(BF16).reshape(nep, CAP // 2, 128)

    def return_copy(k):
        to = lax.rem(ep + k, nep)
        return move(back.at[to], slots.at[ep], e_send.at[k], e_recv.at[k], device(to, tp))

    returns = [return_copy(k) for k in range(1, nep)]
    for c in returns:
        c.start()
        sent.append(c)
    slots[ep] = back[ep]

    own_ids = rows[ep, CAP : CAP + 16, :].astype(F32)
    experts_all = copies.shape[1]
    which = iota((experts_all, GROUP), 0).astype(F32)
    named = [jnp.broadcast_to(own_ids[k : k + 1, :], (experts_all, GROUP)) == which for k in range(2)]
    own_before = rank_before(named[0].astype(F32) + named[1].astype(F32))
    score = logits[...]
    chosen = [jnp.sum(jnp.where(m, score, 0.0), axis=0, keepdims=True) for m in named]
    ranks = [jnp.sum(jnp.where(m, own_before, 0.0), axis=0, keepdims=True) for m in named]
    own_copies = copies[pl.ds(ep, 1), :]
    own_aims = [
        sum(
            jnp.where(own_ids[k : k + 1, :] == float(e), own_copies[:, e : e + 1], 0.0)
            for e in range(experts_all)
        )
        for k in range(2)
    ]
    half_cap = float(CAP // 2)
    places_own = [
        jnp.where(r >= half_cap, float(nep) * half_cap - half_cap, 0.0) + t * half_cap + r
        for r, t in zip(ranks, own_aims)
    ]
    shares = [
        1.0 / (1.0 + jnp.exp(chosen[1] - chosen[0])),
        1.0 / (1.0 + jnp.exp(chosen[0] - chosen[1])),
    ]
    columns = jnp.concatenate(places_own + shares + [jnp.zeros((4, GROUP), F32)], axis=0).T
    lane = iota((GROUP, nep * CAP), 1).astype(F32)
    takes = [jnp.where(lane == columns[:, k : k + 1], 1.0, 0.0).astype(BF16) for k in range(2)]

    for k in range(1, nep):
        came = lax.rem(ep + nep - k, nep)
        move(back.at[ep], slots.at[came], e_send.at[k], e_recv.at[k], device(ep, tp)).wait_recv()
    arrived = slots[...].reshape(nep * CAP // 2, 128).astype(F32)
    left_slots = left_half(arrived.shape)
    stacked = jnp.concatenate(
        [jnp.where(left_slots, arrived, 0.0), jnp.where(left_slots, swap(arrived), 0.0)], axis=0
    ).astype(BF16)
    mixture = columns[:, 2:3] * jnp.dot(takes[0], stacked, preferred_element_type=F32)
    mixture = mixture + columns[:, 3:4] * jnp.dot(takes[1], stacked, preferred_element_type=F32)
    own_packed = rows[ep, 0:CAP, :].astype(F32)
    carried = jnp.concatenate([own_packed, swap(own_packed)], axis=0)
    layer = carried + mixture
    for t in range(nt):
        outgoing[t] = layer[t * own_rows : (t + 1) * own_rows, :].astype(BF16)

    def owner_copy(k):
        to = lax.rem(tp + k, nt)
        return move(outgoing.at[to], incoming.at[tp], f_send.at[k], f_recv.at[k], device(ep, to))

    owners = [owner_copy(k) for k in range(1, nt)]
    for c in owners:
        c.start()
        sent.append(c)
    incoming[tp] = outgoing[tp]
    for k in range(1, nt):
        came = lax.rem(tp + nt - k, nt)
        move(outgoing.at[tp], incoming.at[came], f_send.at[k], f_recv.at[k], device(ep, tp)).wait_recv()
    left_own = left_half((own_rows, 128))
    for i in range(nt // 2):
        v0, v1 = incoming[2 * i].astype(F32), incoming[2 * i + 1].astype(F32)
        whole[:, i * 128 : (i + 1) * 128] = jnp.where(left_own, v0, swap(v1))
    value = whole[...]
    layer_out[...] = value.astype(BF16)
    scale = lax.rsqrt(jnp.sum(value * value, axis=1, keepdims=True) * (1.0 / width) + 1e-06)
    next_out[...] = (value * scale * gain_out[...]).astype(BF16)
    for c in sent:
        c.wait_send()


def collect(attn_out, w_out, residual_in, ids, copies, nep, nt):
    vmem = pl.BlockSpec(memory_space=pltpu.VMEM)
    ny = nep // 2
    return pl.pallas_call(
        functools.partial(collect_kernel, nep, nt),
        out_shape=(
            jax.ShapeDtypeStruct((nep, CAP + 16, 128), BF16),
            jax.ShapeDtypeStruct((8, 128), jnp.int32),
        ),
        in_specs=[vmem] * 5,
        out_specs=(vmem, vmem),
        scratch_shapes=[pltpu.SemaphoreType.DMA((2 * ny,)), pltpu.SemaphoreType.DMA((2 * ny,))],
        compiler_params=pltpu.CompilerParams(collective_id=0, has_side_effects=True),
        name="collect",
    )(attn_out, w_out, residual_in, ids, copies)


def experts_call(half_rows, which, nep, nt, rows, copies, logits, gain_in, gain_out, w_gate, w_up, w_down):
    vmem = pl.BlockSpec(memory_space=pltpu.VMEM)
    hbm = pl.BlockSpec(memory_space=pl.ANY)
    width, inner = w_gate.shape[1], w_gate.shape[2]
    nx = NX if nt > 8 else 2
    nz = nt // nx
    hp = half_rows // 2
    a = (hp * 2 // 5) // 32 * 32
    parts = {"a": (0, a), "b": (a, hp - a)}
    own_rows = GROUP // nt
    keys = gather_plan(nz, nx, parts)[0]
    rs_keys = reduce_plan(nz, nx, parts, 0.4)[0]
    land = sum(row_range(parts, k[0], k[2], k[3], {"z": nz, "x": nx}[k[1]])[1] for k in rs_keys)
    dma = pltpu.SemaphoreType.DMA
    out = jax.ShapeDtypeStruct((own_rows, width), BF16)
    return pl.pallas_call(
        functools.partial(expert_kernel, nep, nt, width, half_rows),
        out_shape=(out, out),
        in_specs=[vmem] * 5 + [hbm] * 3,
        out_specs=(vmem, vmem),
        scratch_shapes=[
            pltpu.VMEM((hp, nep * GROUP), BF16),
            pltpu.VMEM((nep * GROUP, 128), BF16),
            pltpu.VMEM((nep * GROUP, 128), BF16),
            pltpu.VMEM((nz, nx, hp, 128), BF16),
            pltpu.VMEM((half_rows, width), BF16),
            pltpu.VMEM((2, width, inner), BF16),
            pltpu.VMEM((2, width, inner), BF16),
            pltpu.VMEM((2, inner, width), BF16),
            pltpu.VMEM((2, half_rows, inner), BF16),
            pltpu.VMEM((nz, nx, hp, 128), BF16),
            pltpu.VMEM((land, 128), BF16),
            pltpu.VMEM((hp, 128), BF16),
            pltpu.VMEM((2, nep * CAP // 2, 2 * half_rows), BF16),
            pltpu.VMEM((2 * half_rows, 128), BF16),
            pltpu.VMEM((2 * half_rows, 128), BF16),
            pltpu.VMEM((nep, CAP // 2, 128), BF16),
            pltpu.VMEM((nep, CAP // 2, 128), BF16),
            pltpu.VMEM((nt, own_rows, 128), BF16),
            pltpu.VMEM((nt, own_rows, 128), BF16),
            pltpu.VMEM((own_rows, width), F32),
            dma((len(keys),)), dma((len(keys),)),
            dma((len(rs_keys),)), dma((len(rs_keys),)),
            dma((3,)), dma((3,)), dma((3,)),
            dma((1,)), dma((1,)),
            dma((nep,)), dma((nep,)),
            dma((nt,)), dma((nt,)),
        ],
        compiler_params=pltpu.CompilerParams(
            collective_id=which, has_side_effects=True, vmem_limit_bytes=60 * 2**20
        ),
        name="experts_%d" % half_rows,
    )(rows, copies, logits, gain_in, gain_out, w_gate, w_up, w_down)


def per_device(sizes, attn_out, residual_in, w_out, gain_in, router_logits, expert_ids, copy_of, w_gate, w_up, w_down, gain_out):
    nt, nep = lax.axis_size("tp"), lax.axis_size("ep")
    copies = copy_of.astype(F32)
    rows, load = collect(attn_out, w_out, residual_in, expert_ids.T, copies, nep, nt)
    operands = (
        rows, copies, router_logits.T, gain_in[None, :], gain_out[None, :], w_gate, w_up, w_down
    )
    branches = [
        functools.partial(experts_call, size, i + 1, nep, nt) for i, size in enumerate(sizes)
    ]
    if len(branches) == 1:
        return branches[0](*operands)
    most = load[0, 0]
    choice = sum((most > 2 * size).astype(jnp.int32) for size in sizes[:-1])
    return lax.switch(choice, branches, *operands)


def solution(mesh, sizes=(512, 640, 1024)):
    return jax.shard_map(
        functools.partial(per_device, sizes),
        mesh=mesh,
        in_specs=(
            P("ep", None),
            P("ep", None),
            P(None, "tp"),
            P(),
            P("ep", None),
            P("ep", None),
            P(),
            P("ep", None, "tp"),
            P("ep", None, "tp"),
            P("ep", "tp", None),
            P(),
        ),
        out_specs=(P(("ep", "tp"), None), P(("ep", "tp"), None)),
        check_vma=False,
    )
```

time: 537 us -> 111 us (0.21)
  the two profiles are of different devices: /device:TPU:8 before, /device:TPU:16 now
where the time goes in v1:
time: 111 us
  Pallas kernels  101 us (91%)
  local copies, waits for them, and re-layouts  7.78 us (7%)
  between operations  2.02 us (2%)
    pallas_call x1, Pallas kernels, experts_call(): pl.pallas_call(functools.partial(expert_kernel, nep, nt, width, half_rows...  84.3 us
    pallas_call x1, Pallas kernels, collect(): pl.pallas_call(functools.partial(collect_kernel, nep, nt), out_shape=(jax...  16.6 us
    unnamed x16, local copies, waits for them, and re-layouts  4.02 us
    another operation x2, local copies, waits for them, and re-layouts  2.56 us

profile of v1, /device:TPU:16, one launch (start us, length us, event | category | flops | bytes accessed | tf_op | source)
XLA Modules:
  0.0 111.1 jit_solution(6674961091631583740)
XLA Ops:
  0.6 0.8 copy.34
  1.4 0.0 copy-start.2
  1.4 2.0 %copy.35.w_out = bf16[2048,64]{1,0:T(8,128)(2,1)} copy(bf16[2048,64]{0,1:T(8,128)(2,1)} %param.16) | data formatting | bytes 524288 | tf_op args[2]
  3.4 0.0 copy-start
  3.4 0.0 copy-start.1
  3.4 0.0 copy-start.5
  3.4 16.6 %collect.1 = (bf16[16,80,128]{2,1,0:T(8,128)(2,1)S(1)}, s32[8,128]{1,0:T(8,128)}) custom-call(bf16[128,2048]{1,0:T(8,128)(2,1)} %attn.1, bf16[2048,64]{1,0:T(8,128)(2,1)} %copy.35.w_out, bf16[128,2048]{1,0:T(8,128)(2,1)} %residual.1, s32[2,128]{1,0:T(2,128)} %bitcast.18, f32[16,8]{1,0:T(8,128)S(1)} %convert_element_type.11.copies), custom_call_target="tpu_custom_call" | custom-call | tf_op jit(solution)/shard_map/collect/pallas_call | solution.py:530
  20.0 0.0 copy-start.4
  20.0 0.0 copy-start.3
  20.0 1.2 %slice.3 = s32[1,1]{1,0:T(1,128)} slice(s32[8,128]{1,0:T(8,128)} %get-tuple-element.76), slice={[0:1], [0:1]} | slice | bytes 8 | tf_op jit(solution)/shard_map/slice | solution.py:611
  22.5 0.0 copy-done.2
  22.5 0.0 copy-done
  22.6 0.0 copy-done.1
  22.6 0.0 copy-done.5
  22.6 0.0 copy-done.4
  22.6 0.0 copy-done.3
  22.6 87.3 %conditional.1 = ((bf16[4,2048]{1,0:T(4,128)(2,1)S(1)}, bf16[4,2048]{1,0:T(4,128)(2,1)S(1)})) conditional(s32[]{:T(128)} %bitcast.7, (bf16[16,80,128]{2,1,0:T(8,128)(2,1)S(1)}, f32[16,8]{1,0:T(8,128)S(1)}, f32[8,128]{1,0:T(8,128)S(1)}, f32[2048]{0:T(1024)S(1)}, f32[2048]{0:T(1024)S(1)}, ...), branch_computations={%region_0.0_spmd, %region_1.0_spmd, %region_2.0_spmd} | conditional | bytes 2883592 | solution.py:613
  22.8 1.3 %copy.39.w_up = bf16[1,2048,176]{2,1,0:T(8,128)(2,1)} copy(bf16[1,2048,176]{1,2,0:T(8,128)(2,1)S(1)} %get-tuple-element.136) | data formatting | bytes 1441792 | tf_op jit(solution)/shard_map
  24.1 1.3 %copy.38.w_gate = bf16[1,2048,176]{2,1,0:T(8,128)(2,1)} copy(bf16[1,2048,176]{1,2,0:T(8,128)(2,1)S(1)} %get-tuple-element.135) | data formatting | bytes 1441792 | tf_op jit(solution)/shard_map
  25.4 84.3 %experts_640.1 = (bf16[4,2048]{1,0:T(4,128)(2,1)S(1)}, bf16[4,2048]{1,0:T(4,128)(2,1)S(1)}) custom-call(bf16[16,80,128]{2,1,0:T(8,128)(2,1)S(1)} %get-tuple-element.56.rows, f32[16,8]{1,0:T(8,128)S(1)} %get-tuple-element.57.copies, f32[8,128]{1,0:T(8,128)S(1)} %get-tuple-element.58.logits, f32[1,2048]{1,0:T(1,128)S(1)} %bitcast.10, f32[1,2048]{1,0:T(1,128)S(1)} %bitcast.13, ...), custom_call_target="tpu_custom_call" | custom-call | tf_op jit(solution)/shard_map/cond/branch_1_fun/experts_640/pallas_call | solution.py:559
  109.9 0.6 copy.50
  110.5 0.6 copy.51
  (1 shorter events, 0.0 us)
Async XLA Ops:
  1.4 21.1 %copy-start.2 = (bf16[1,176,2048]{2,1,0:T(8,128)(2,1)S(1)}, bf16[1,176,2048]{2,1,0:T(8,128)(2,1)}, u32[]{:S(2)}) copy-start(bf16[1,176,2048]{2,1,0:T(8,128)(2,1)} %param.23) | copy-start | bytes 2162692
  3.4 19.1 %copy-start = (bf16[1,2048,176]{1,2,0:T(8,128)(2,1)S(1)}, bf16[1,2048,176]{1,2,0:T(8,128)(2,1)}, u32[]{:S(2)}) copy-start(bf16[1,2048,176]{1,2,0:T(8,128)(2,1)} %param.21) | copy-start | bytes 2162692
  3.4 19.1 %copy-start.1 = (bf16[1,2048,176]{1,2,0:T(8,128)(2,1)S(1)}, bf16[1,2048,176]{1,2,0:T(8,128)(2,1)}, u32[]{:S(2)}) copy-start(bf16[1,2048,176]{1,2,0:T(8,128)(2,1)} %param.22) | copy-start | bytes 2162692
  3.4 19.2 %copy-start.5 = (f32[128,8]{0,1:T(8,128)S(1)}, f32[128,8]{0,1:T(8,128)}, u32[]{:S(2)}) copy-start(f32[128,8]{0,1:T(8,128)} %param.18) | copy-start | bytes 12292
  20.0 2.6 %copy-start.4 = (f32[2048]{0:T(1024)S(1)}, f32[2048]{0:T(1024)}, u32[]{:S(2)}) copy-start(f32[2048]{0:T(1024)} %param.24) | copy-start | bytes 24580
  20.0 2.6 %copy-start.3 = (f32[2048]{0:T(1024)S(1)}, f32[2048]{0:T(1024)}, u32[]{:S(2)}) copy-start(f32[2048]{0:T(1024)} %param.17) | copy-start | bytes 24580

commit v2 on v0

v2 whole, which is shorter than its diff:
```python
import functools
import heapq

import jax
import jax.numpy as jnp
from jax import lax
from jax.experimental import pallas as pl
from jax.experimental.pallas import tpu as pltpu
from jax.sharding import PartitionSpec as P

MESH = pl.DeviceIdType.MESH
F32 = jnp.float32
BF16 = jnp.bfloat16
NX = 4
COLS = 64
GROUP = 128
CAP = 64
SIGNS = (1, -1)


def row_range(parts, part, sign, dist, count):
    start, size = parts[part]
    if 2 * dist == count:
        half = size // 2
        return (start, half) if sign > 0 else (start + half, half)
    return (start, size)


def split_rows(half, pieces):
    units, out, at, taken = half // 32, [], 0, 0
    for i in range(pieces):
        size = (units * (i + 1) // pieces) * 32 - at
        first = int(0.41 * (at + size) / 32 + 0.5) * 32 - taken
        first = min(max(first, 32), size - 32)
        out.append((at, first, size - first))
        at, taken = at + size, taken + first
    return out


def part_of(pieces, u):
    start, first, second = pieces[u]
    return {"a": (start, first), "b": (start + first, second)}


def gather_sends(nz, nx, pieces, u):
    count, parts, sends = {"z": nz, "x": nx}, part_of(pieces, u), {}
    for part, (first, second) in (("a", ("x", "z")), ("b", ("z", "x"))):
        for axis in (first, second):
            n = count[axis]
            for other in range(1 if axis == first else count[first]):
                for dist in range(1, n // 2 + 1):
                    for sign in SIGNS:
                        need = set()
                        if dist > 1:
                            need.add(("g", u, part, axis, sign, dist - 1, other))
                        elif axis == second and other:
                            m = count[first]
                            if 2 * other <= m:
                                need.add(("g", u, part, first, 1, other, 0))
                            if 2 * other >= m:
                                need.add(("g", u, part, first, -1, m - other, 0))
                        size = row_range(parts, part, sign, dist, n)[1]
                        sends[("g", u, part, axis, sign, dist, other)] = ((axis, sign), size, need)
    return sends


def reduce_sends(nz, nx, pieces, u):
    count, parts, sends = {"z": nz, "x": nx}, part_of(pieces, u), {}
    for part, (first, second) in (("a", ("z", "x")), ("b", ("x", "z"))):
        for axis in (first, second):
            n = count[axis]
            for other in range(count[second] if axis == first else 1):
                for dist in range(n // 2, 0, -1):
                    for sign in SIGNS:
                        offset = (sign * dist) % n
                        need = {("c", u, offset if axis == "z" else other)}
                        if 2 * dist < n:
                            need.add(("r", u, part, axis, sign, dist + 1, other))
                        if axis == second:
                            for way in SIGNS:
                                need.add(("r", u, part, first, way, 1, offset))
                        size = row_range(parts, part, sign, dist, n)[1]
                        sends[("r", u, part, axis, sign, dist, other)] = ((axis, sign), size, need)
    return sends


def schedule(nz, nx, pieces):
    rate, latency = 181.0, 1.7
    sends, tasks, landing, total = {}, {}, {}, 0
    far = sorted(range(nz), key=lambda d: (-min(d, nz - d), d))
    for u, (_, first, second) in enumerate(pieces):
        gathers = gather_sends(nz, nx, pieces, u)
        reduces = reduce_sends(nz, nx, pieces, u)
        sends.update(gathers)
        sends.update(reduces)
        rows = first + second
        tasks[("x", u)] = (rows * 0.011, set(gathers))
        before = ("x", u)
        for dz in far:
            tasks[("c", u, dz)] = (rows * 0.0007, {before})
            before = ("c", u, dz)
        for key, value in reduces.items():
            landing[key] = (total, value[1])
            total += value[1]
    done, free, ops, arrivals = set(), {}, [], []
    waiting, later, now = dict(sends), dict(tasks), 0.0

    def release():
        for key in [k for k, v in waiting.items() if v[2] <= done]:
            link, size, _ = waiting.pop(key)
            free[link] = max(now, free.get(link, 0.0)) + size / rate
            ops.append(("start", key))
            heapq.heappush(arrivals, (free[link] + latency, len(ops), key))

    release()
    while arrivals or later:
        if arrivals and arrivals[0][0] <= now:
            key = heapq.heappop(arrivals)[2]
            ops.append(("wait", key))
            now += 0.05 + (sends[key][1] * 0.0006 if key[0] == "r" else 0.0)
            done.add(key)
            release()
            continue
        able = [k for k, v in later.items() if v[1] <= done]
        if able:
            now += later.pop(able[0])[0]
            ops.append(("task", able[0]))
            done.add(able[0])
            release()
            continue
        now = max(now, arrivals[0][0])
    assert not waiting
    return {key: i for i, key in enumerate(sends)}, ops, landing, total


def iota(shape, dim):
    return lax.broadcasted_iota(jnp.int32, shape, dim)


def left_half(shape):
    return iota(shape, len(shape) - 1) < COLS


def swap(value):
    return pltpu.roll(value, COLS, value.ndim - 1)


def rank_before(hits):
    tri = (iota((GROUP, GROUP), 0) < iota((GROUP, GROUP), 1)).astype(F32).astype(BF16)
    return jnp.dot(hits.astype(BF16), tri, preferred_element_type=F32)


def targets_of(ids, copies):
    experts = copies.shape[1]
    total = jnp.zeros(ids.shape, F32)
    for e in range(experts):
        total = total + jnp.where(ids == float(e), copies[:, e : e + 1], 0.0)
    return total


def contract(lhs, rhs):
    return lax.dot_general(lhs, rhs, (((1,), (1,)), ((), ())), preferred_element_type=F32)


def collect_kernel(
    nep, nt, sizes,
    attn, w_out, residual, ids, copies,
    rows_out, names_out, aims_out, choice,
    columns, by_group, local_sem, send_sem, recv_sem,
):
    ep, tp = lax.axis_index("ep"), lax.axis_index("tp")
    ny = nep // 2
    y, core = ep // 2, lax.rem(ep, 2)

    barrier = pltpu.get_barrier_semaphore()
    for k in range(1, nep):
        pl.semaphore_signal(
            barrier, inc=1, device_id={"ep": lax.rem(ep + k, nep), "tp": tp}, device_id_type=MESH
        )
    fetch = pltpu.make_async_copy(
        residual.at[:, pl.ds(pl.multiple_of((tp // 2) * 128, 128), 128)], columns, local_sem.at[0]
    )
    fetch.start()
    names = ids[...].astype(F32)
    names_out[core, y] = jnp.concatenate([names, jnp.zeros((14, GROUP), F32)], axis=0).astype(BF16)
    experts = copies.shape[0]
    padded = jnp.concatenate([copies[...].astype(F32), jnp.zeros((experts, 128 - nep), F32)], axis=1)
    if experts < 8:
        padded = jnp.concatenate([padded, jnp.zeros((8 - experts, 128), F32)], axis=0)
    by_group[...] = padded.T
    product = contract(attn[...], w_out[...]).astype(BF16).astype(F32)
    fetch.wait()
    pair = columns[...].astype(F32)
    left = left_half((CAP, 128))
    pair = jnp.where(lax.rem(tp, 2) == 1, swap(pair), pair)
    carried = pair + jnp.concatenate([product, product], axis=1)
    packed = jnp.where(left, carried[:CAP], swap(carried[CAP:]))
    rows_out[y] = packed.astype(BF16)

    pl.semaphore_wait(barrier, nep - 1)

    def send_names(k, parity, plane):
        return pltpu.make_async_remote_copy(
            src_ref=names_out.at[parity, plane],
            dst_ref=names_out.at[parity, plane],
            send_sem=send_sem.at[k],
            recv_sem=recv_sem.at[k],
            device_id={"ep": lax.rem(ep + k, nep), "tp": tp},
            device_id_type=MESH,
        )

    def send_rows(k, plane):
        return pltpu.make_async_remote_copy(
            src_ref=rows_out.at[plane],
            dst_ref=rows_out.at[plane],
            send_sem=send_sem.at[nep + k],
            recv_sem=recv_sem.at[nep + k],
            device_id={"ep": 2 * lax.rem(y + k, ny) + core, "tp": tp},
            device_id_type=MESH,
        )

    sent = [send_names(k, core, y) for k in sorted(range(1, nep), key=lambda k: -min(k, nep - k))]
    sent += [send_rows(k, y) for k in sorted(range(1, ny), key=lambda k: -min(k, ny - k))]
    for c in sent:
        c.start()
    for k in range(1, nep):
        came = lax.rem(ep + nep - k, nep)
        send_names(k, lax.rem(came, 2), came // 2).wait_recv()

    table = names_out[...].astype(F32)
    by_copy = [by_group[pl.ds(p, ny, stride=2), :] for p in range(2)]
    hits = [jnp.zeros((ny, GROUP), F32) for p in range(2)]
    most = jnp.zeros((1, 128), F32)
    lane = iota((ny, 128), 1)
    for p in range(2):
        aims = [targets_of(table[p, :, k, :], by_copy[p][:, :experts]) for k in range(2)]
        for k in range(2):
            aims_out[k, p] = aims[k]
        sums = jnp.zeros((ny, 128), F32)
        for q in range(ny):
            low, high = float(2 * q), float(2 * q + 1)
            hit = sum(((v >= low) & (v <= high)).astype(F32) for v in aims)
            sums = sums + jnp.where(lane == q, jnp.sum(hit, axis=1, keepdims=True), 0.0)
        most = jnp.maximum(most, jnp.sum(sums, axis=0, keepdims=True))
    largest = jnp.max(most).astype(jnp.int32)
    choice[0] = sum((largest > size).astype(jnp.int32) for size in sizes[:-1]) + 0 * largest

    for k in range(1, ny):
        send_rows(k, lax.rem(y + ny - k, ny)).wait_recv()
    for c in sent:
        c.wait_send()


def expert_kernel(
    nep, nt, width, size, count_pieces,
    rows, names, aims, logits, gain_in, gain_out, w_gate, w_up, w_down,
    layer_out, next_out,
    pick, flat_l, flat_r, spots, got, full, gates, ups, downs, hid, share, landed, ret_pick, ret_start,
    ret_l, ret_r, back, slots, outgoing, incoming, whole,
    t_send, t_recv, w_local, w_send, w_recv, e_send, e_recv, f_send, f_recv,
):
    ep, tp = lax.axis_index("ep"), lax.axis_index("tp")
    nx = NX if nt > 8 else 2
    nz = nt // nx
    ny = nep // 2
    y, core = ep // 2, lax.rem(ep, 2)
    mate = 2 * y + (1 - core)
    z, x = tp // nx, lax.rem(tp, nx)
    hp = size // 2
    pieces = split_rows(hp, count_pieces)
    own_rows = GROUP // nt
    count = {"z": nz, "x": nx}

    def neighbour(axis, sign):
        if axis == "z":
            return {"ep": ep, "tp": lax.rem(z + sign + nz, nz) * nx + x}
        return {"ep": ep, "tp": z * nx + lax.rem(x + sign + nx, nx)}

    def plane_peer(k):
        return {"ep": 2 * lax.rem(y + k, ny) + core, "tp": tp}

    partner = {"ep": mate, "tp": tp}
    friends = [neighbour(axis, sign) for axis in ("z", "x") for sign in SIGNS] + [partner]
    friends += [plane_peer(k) for k in range(1, ny)]
    barrier = pltpu.get_barrier_semaphore()
    for friend in friends:
        pl.semaphore_signal(barrier, inc=1, device_id=friend, device_id_type=MESH)

    def move(src, dst, send, recv, where):
        return pltpu.make_async_remote_copy(
            src_ref=src, dst_ref=dst, send_sem=send, recv_sem=recv, device_id=where, device_id_type=MESH
        )

    weights = ((w_gate, gates), (w_up, ups), (w_down, downs))
    own_weights = [
        pltpu.make_async_copy(src.at[0], dst.at[0], w_local.at[i]) for i, (src, dst) in enumerate(weights)
    ]
    for c in own_weights:
        c.start()

    low = (2 * y).astype(F32)
    aim = [aims[k, core] for k in range(2)]
    hits = [sum((v == low + c).astype(F32) for v in aim) for c in (0.0, 1.0)]
    totals = [jnp.sum(h, axis=1, keepdims=True) for h in hits]
    lower = (iota((ny, ny), 1) < iota((ny, ny), 0)).astype(F32).astype(BF16)
    offsets = [
        jnp.dot(lower, jnp.broadcast_to(t, (ny, 128)).astype(BF16), preferred_element_type=F32)
        for t in totals
    ]
    count_low = jnp.sum(totals[0], axis=0, keepdims=True)
    starts = [offsets[0], offsets[1] + count_low]
    places = [starts[c] + rank_before(hits[c]) for c in range(2)]
    for k in range(2):
        spots[k] = jnp.where(
            aim[k] == low, places[0], jnp.where(aim[k] == low + 1.0, places[1], -1.0)
        )
    for c in range(2):
        ret_start[c] = starts[c]

    left64 = left_half((CAP, 128))

    def flatten(g, carry):
        packed = rows[g].astype(F32)
        other = swap(packed)
        top = pl.ds(pl.multiple_of(g * GROUP, GROUP), CAP)
        bottom = pl.ds(pl.multiple_of(g * GROUP + CAP, CAP), CAP)
        flat_l[top, :] = jnp.where(left64, packed, 0.0).astype(BF16)
        flat_l[bottom, :] = jnp.where(left64, other, 0.0).astype(BF16)
        flat_r[top, :] = jnp.where(left64, 0.0, other).astype(BF16)
        flat_r[bottom, :] = jnp.where(left64, 0.0, packed).astype(BF16)
        return carry

    lax.fori_loop(0, ny, flatten, 0)

    def choose(q):
        line = iota((hp, 128), 0).astype(F32) + float(q * hp)

        def one(g, carry):
            hit = (spots[0, pl.ds(g, 1), :] == line) | (spots[1, pl.ds(g, 1), :] == line)
            lanes = pl.ds(pl.multiple_of(g * GROUP, GROUP), GROUP)
            pick[:, lanes] = jnp.where(hit, 1.0, 0.0).astype(BF16)
            return carry

        lax.fori_loop(0, ny, one, 0)
        return jnp.dot(pick[...], (flat_l, flat_r)[q][...], preferred_element_type=F32)

    got[0, 0] = choose(0).astype(BF16)
    got[0, 0] = (got[0, 0].astype(F32) + choose(1)).astype(BF16)

    pl.semaphore_wait(barrier, len(friends))

    mate_weights = [
        move(src.at[0], dst.at[1], w_send.at[i], w_recv.at[i], partner)
        for i, (src, dst) in enumerate(weights)
    ]

    def slot_of(axis, offset, other):
        return (offset % nz, other) if axis == "z" else (other, offset % nx)

    index, ops, landing, _ = schedule(nz, nx, pieces)

    def transfer(key):
        kind, u, part, axis, sign, dist, other = key
        start, many = row_range(part_of(pieces, u), part, sign, dist, count[axis])
        i = index[key]
        if kind == "g":
            src, dst = slot_of(axis, sign * (dist - 1), other), slot_of(axis, sign * dist, other)
            target = got.at[dst[0], dst[1], pl.ds(start, many), :]
            source = got.at[src[0], src[1], pl.ds(start, many), :]
        else:
            src = slot_of(axis, sign * dist, other)
            target = landed.at[pl.ds(landing[key][0], many), :]
            source = share.at[src[0], src[1], pl.ds(start, many), :]
        return move(source, target, t_send.at[i], t_recv.at[i], neighbour(axis, sign))

    def add_landed(key):
        _, u, part, axis, sign, dist, other = key
        start, many = row_range(part_of(pieces, u), part, sign, dist, count[axis])
        at = slot_of(axis, sign * (dist - 1), other)
        here, there = pl.ds(start, many), pl.ds(landing[key][0], many)
        share[at[0], at[1], here, :] = (
            share[at[0], at[1], here, :].astype(F32) + landed[there, :].astype(F32)
        ).astype(BF16)

    core_f = core.astype(F32)

    def experts(u):
        start, many = pieces[u][0], pieces[u][1] + pieces[u][2]
        at = 2 * start
        here = pl.ds(start, many)
        left = left_half((many, 128))

        def join(i, carry):
            p0, p1 = [
                got[
                    lax.rem(z - t // nx + nz, nz), lax.rem(x - lax.rem(t, nx) + nx, nx), here, :
                ].astype(F32)
                for t in (2 * i, 2 * i + 1)
            ]
            lanes = pl.ds(pl.multiple_of(i * 128, 128), 128)
            full[at : at + many, lanes] = jnp.where(left, p0, swap(p1)).astype(BF16)
            full[at + many : at + 2 * many, lanes] = jnp.where(left, swap(p0), p1).astype(BF16)
            return carry

        lax.fori_loop(0, nt // 2, join, 0)
        tile = next(t for t in (128, 96, 160, 64, 32) if many % t == 0)
        sides = many // tile

        def one(i, carry):
            span = pl.ds(pl.multiple_of(at + i * tile, 32), tile)
            value = full[span, :].astype(F32)
            scale = lax.rsqrt(jnp.sum(value * value, axis=1, keepdims=True) * (1.0 / width) + 1e-06)
            normed = (value * scale * gain_in[...]).astype(BF16)
            first = start + lax.rem(i, sides) * tile + (i // sides) * hp
            spot = (iota((tile, 1), 0) + first).astype(F32)
            in_low = (spot < jnp.broadcast_to(count_low, (tile, 1))).astype(F32)
            mine = in_low * (1.0 - core_f) + (1.0 - in_low) * core_f
            for w, keep in ((0, mine), (1, 1.0 - mine)):
                gate = contract(normed, gates[w])
                up = contract(normed, ups[w])
                value_h = gate / (1.0 + jnp.exp(-gate)) * up
                hid[w, span, :] = jnp.where(keep > 0.5, value_h, 0.0).astype(BF16)
            return carry

        lax.fori_loop(0, 2 * sides, one, 0)

    def down(u, dz):
        start, many = pieces[u][0], pieces[u][1] + pieces[u][2]
        left = left_half((many, 128))
        lanes = pl.ds(pl.multiple_of(lax.rem(z + dz, nz) * (nx * COLS), 128), nx * COLS)
        wd = [downs[w, :, lanes] for w in range(2)]
        sides = []
        for q in range(2):
            at = slice(2 * start + q * many, 2 * start + (q + 1) * many)
            sides.append(
                jnp.dot(hid[0, at, :], wd[0], preferred_element_type=F32)
                + jnp.dot(hid[1, at, :], wd[1], preferred_element_type=F32)
            )
        here = pl.ds(start, many)
        for i in range(nx // 2):
            top, bottom = [v[:, i * 128 : (i + 1) * 128] for v in sides]
            d0 = lax.rem(2 * i - x + nx, nx)
            d1 = lax.rem(2 * i + 1 - x + nx, nx)
            share[dz, d0, here, :] = jnp.where(left, top, swap(bottom)).astype(BF16)
            share[dz, d1, here, :] = jnp.where(left, swap(top), bottom).astype(BF16)

    sent = list(mate_weights)
    for c in mate_weights:
        c.start()
    have_weights = False
    for kind, key in ops:
        if kind == "task":
            if key[0] == "x":
                if not have_weights:
                    have_weights = True
                    for c in own_weights:
                        c.wait()
                    for c in mate_weights:
                        c.wait_recv()
                experts(key[1])
            else:
                down(key[1], key[2])
            continue
        c = transfer(key)
        if kind == "start":
            c.start()
            sent.append(c)
        else:
            c.wait_recv()
            if key[0] == "r":
                add_landed(key)

    left = left_half((hp, 128))
    half_cap = CAP // 2
    lead = (iota((half_cap, size), 1) - iota((half_cap, size), 0)).astype(F32)
    for q in range(2):
        for c in range(2):

            def mark(g, carry, q=q, c=c):
                first = ret_start[c, pl.ds(g, 1), 0:1] + float(q * half_cap)
                at = pl.ds(pl.multiple_of(g * CAP + c * half_cap, half_cap), half_cap)
                ret_pick[q, at, :] = jnp.where(lead == first, 1.0, 0.0).astype(BF16)
                return carry

            lax.fori_loop(0, ny, mark, 0)
    v = share[0, 0].astype(F32)
    w = swap(v)
    ret_l[0:hp, :] = jnp.where(left, v, 0.0).astype(BF16)
    ret_l[hp : 2 * hp, :] = jnp.where(left, w, 0.0).astype(BF16)
    ret_r[0:hp, :] = jnp.where(left, 0.0, w).astype(BF16)
    ret_r[hp : 2 * hp, :] = jnp.where(left, 0.0, v).astype(BF16)
    blocks = jnp.dot(ret_pick[0], ret_l[...], preferred_element_type=F32)
    blocks = blocks + jnp.dot(ret_pick[1], ret_r[...], preferred_element_type=F32)
    back[...] = blocks.astype(BF16).reshape(ny, CAP, 128)

    def return_copy(k, to, came):
        return move(back.at[to], slots.at[came], e_send.at[k], e_recv.at[k], plane_peer(k))

    returns = [
        return_copy(k, lax.rem(y + k, ny), y)
        for k in sorted(range(1, ny), key=lambda k: -min(k, ny - k))
    ]
    for c in returns:
        c.start()
        sent.append(c)
    slots[y] = back[y]

    own_ids = names[core, y].astype(F32)
    experts_all = logits.shape[0]
    which = iota((experts_all, GROUP), 0).astype(F32)
    named = [jnp.broadcast_to(own_ids[k : k + 1, :], (experts_all, GROUP)) == which for k in range(2)]
    own_before = rank_before(named[0].astype(F32) + named[1].astype(F32))
    score = logits[...]
    chosen = [jnp.sum(jnp.where(m, score, 0.0), axis=0, keepdims=True) for m in named]
    ranks = [jnp.sum(jnp.where(m, own_before, 0.0), axis=0, keepdims=True) for m in named]
    own_aims = [aims[k, core, pl.ds(y, 1), :] for k in range(2)]
    places_own = [
        jnp.where(r >= float(half_cap), float((nep - 1) * half_cap), 0.0) + t * float(half_cap) + r
        for r, t in zip(ranks, own_aims)
    ]
    shares = [
        1.0 / (1.0 + jnp.exp(chosen[1] - chosen[0])),
        1.0 / (1.0 + jnp.exp(chosen[0] - chosen[1])),
    ]
    table = jnp.concatenate(places_own + shares + [jnp.zeros((4, GROUP), F32)], axis=0).T
    lane = iota((GROUP, nep * CAP), 1).astype(F32)
    takes = [jnp.where(lane == table[:, k : k + 1], 1.0, 0.0).astype(BF16) for k in range(2)]

    for k in range(1, ny):
        return_copy(k, y, lax.rem(y + ny - k, ny)).wait_recv()
    arrived = slots[...].reshape(ny * CAP, 128).astype(F32)
    left_slots = left_half(arrived.shape)
    stacked = jnp.concatenate(
        [jnp.where(left_slots, arrived, 0.0), jnp.where(left_slots, swap(arrived), 0.0)], axis=0
    ).astype(BF16)
    mixture = table[:, 2:3] * jnp.dot(takes[0], stacked, preferred_element_type=F32)
    mixture = mixture + table[:, 3:4] * jnp.dot(takes[1], stacked, preferred_element_type=F32)
    own_packed = rows[y].astype(F32)
    layer = jnp.concatenate([own_packed, swap(own_packed)], axis=0) + mixture
    for t in range(nt):
        outgoing[t] = layer[t * own_rows : (t + 1) * own_rows, :].astype(BF16)

    def owner_copy(k, to, came):
        where = {"ep": ep, "tp": lax.rem(tp + k, nt)}
        return move(outgoing.at[to], incoming.at[came], f_send.at[k], f_recv.at[k], where)

    def hops(k):
        return min(k // nx, nz - k // nx) + min(k % nx, nx - k % nx)

    owners = [
        owner_copy(k, lax.rem(tp + k, nt), tp) for k in sorted(range(1, nt), key=lambda k: -hops(k))
    ]
    for c in owners:
        c.start()
        sent.append(c)
    incoming[tp] = outgoing[tp]
    for k in range(1, nt):
        owner_copy(k, tp, lax.rem(tp + nt - k, nt)).wait_recv()
    left_own = left_half((own_rows, 128))
    for i in range(nt // 2):
        v0, v1 = incoming[2 * i].astype(F32), incoming[2 * i + 1].astype(F32)
        whole[:, i * 128 : (i + 1) * 128] = jnp.where(left_own, v0, swap(v1))
    value = whole[...]
    layer_out[...] = value.astype(BF16)
    scale = lax.rsqrt(jnp.sum(value * value, axis=1, keepdims=True) * (1.0 / width) + 1e-06)
    next_out[...] = (value * scale * gain_out[...]).astype(BF16)
    for c in sent:
        c.wait_send()


def collect(attn_out, w_out, residual_in, ids, copies, nep, nt, sizes):
    vmem = pl.BlockSpec(memory_space=pltpu.VMEM)
    ny = nep // 2
    dma = pltpu.SemaphoreType.DMA
    return pl.pallas_call(
        functools.partial(collect_kernel, nep, nt, sizes),
        out_shape=(
            jax.ShapeDtypeStruct((ny, CAP, 128), BF16),
            jax.ShapeDtypeStruct((2, ny, 16, 128), BF16),
            jax.ShapeDtypeStruct((2, 2, ny, 128), F32),
            jax.ShapeDtypeStruct((1,), jnp.int32),
        ),
        in_specs=[vmem, vmem, pl.BlockSpec(memory_space=pl.ANY), vmem, vmem],
        out_specs=(vmem, vmem, vmem, pl.BlockSpec(memory_space=pltpu.SMEM)),
        scratch_shapes=[
            pltpu.VMEM((GROUP, 128), BF16),
            pltpu.VMEM((128, 8), F32),
            dma((1,)),
            dma((nep + ny,)),
            dma((nep + ny,)),
        ],
        compiler_params=pltpu.CompilerParams(collective_id=0, has_side_effects=True),
        name="collect",
    )(attn_out, w_out, residual_in, ids, copies)


def experts_call(size, which, pieces, nep, nt, rows, names, aims, logits, gain_in, gain_out, w_gate, w_up, w_down):
    vmem = pl.BlockSpec(memory_space=pltpu.VMEM)
    hbm = pl.BlockSpec(memory_space=pl.ANY)
    inner, width = w_gate.shape[1], w_gate.shape[2]
    nx = NX if nt > 8 else 2
    nz = nt // nx
    ny = nep // 2
    hp = size // 2
    own_rows = GROUP // nt
    index, _, _, land = schedule(nz, nx, split_rows(hp, pieces))
    dma = pltpu.SemaphoreType.DMA
    out = jax.ShapeDtypeStruct((own_rows, width), BF16)
    return pl.pallas_call(
        functools.partial(expert_kernel, nep, nt, width, size, pieces),
        out_shape=(out, out),
        in_specs=[vmem] * 6 + [hbm] * 3,
        out_specs=(vmem, vmem),
        scratch_shapes=[
            pltpu.VMEM((hp, ny * GROUP), BF16),
            pltpu.VMEM((ny * GROUP, 128), BF16),
            pltpu.VMEM((ny * GROUP, 128), BF16),
            pltpu.VMEM((2, ny, 128), F32),
            pltpu.VMEM((nz, nx, hp, 128), BF16),
            pltpu.VMEM((size, width), BF16),
            pltpu.VMEM((2, inner, width), BF16),
            pltpu.VMEM((2, inner, width), BF16),
            pltpu.VMEM((2, inner, width), BF16),
            pltpu.VMEM((2, size, inner), BF16),
            pltpu.VMEM((nz, nx, hp, 128), BF16),
            pltpu.VMEM((land, 128), BF16),
            pltpu.VMEM((2, ny * CAP, size), BF16),
            pltpu.VMEM((2, ny, 128), F32),
            pltpu.VMEM((size, 128), BF16),
            pltpu.VMEM((size, 128), BF16),
            pltpu.VMEM((ny, CAP, 128), BF16),
            pltpu.VMEM((ny, CAP, 128), BF16),
            pltpu.VMEM((nt, own_rows, 128), BF16),
            pltpu.VMEM((nt, own_rows, 128), BF16),
            pltpu.VMEM((own_rows, width), F32),
            dma((len(index),)), dma((len(index),)),
            dma((3,)), dma((3,)), dma((3,)),
            dma((ny,)), dma((ny,)),
            dma((nt,)), dma((nt,)),
        ],
        compiler_params=pltpu.CompilerParams(
            collective_id=which, has_side_effects=True, vmem_limit_bytes=60 * 2**20
        ),
        name="experts_%d" % size,
    )(rows, names, aims, logits, gain_in, gain_out, w_gate, w_up, w_down)


def per_device(sizes, attn_out, residual_in, w_out, gain_in, router_logits, expert_ids, copy_of, w_gate, w_up, w_down, gain_out):
    nt, nep = lax.axis_size("tp"), lax.axis_size("ep")
    rows, names, aims, choice = collect(
        attn_out, w_out.T, residual_in, expert_ids.T, copy_of.T, nep, nt, tuple(s for s, _ in sizes)
    )
    operands = (
        rows, names, aims, router_logits.T, gain_in[None, :], gain_out[None, :],
        jnp.swapaxes(w_gate, 1, 2), jnp.swapaxes(w_up, 1, 2), w_down,
    )
    branches = [
        functools.partial(experts_call, size, i + 1, pieces, nep, nt)
        for i, (size, pieces) in enumerate(sizes)
    ]
    if len(branches) == 1:
        return branches[0](*operands)
    return lax.switch(choice[0], branches, *operands)


def solution(mesh, sizes=((512, 1), (640, 1), (1024, 1))):
    return jax.shard_map(
        functools.partial(per_device, sizes),
        mesh=mesh,
        in_specs=(
            P("ep", None),
            P("ep", None),
            P(None, "tp"),
            P(),
            P("ep", None),
            P("ep", None),
            P(),
            P("ep", None, "tp"),
            P("ep", None, "tp"),
            P("ep", "tp", None),
            P(),
        ),
        out_specs=(P(("ep", "tp"), None), P(("ep", "tp"), None)),
        check_vma=False,
    )
```

time: 537 us -> 132 us (0.25)
  waiting for transfers between devices: 305 us -> 0 us
  blocking collectives: 171 us -> 0 us
  Pallas kernels: 0 us -> 122 us
  local copies, waits for them, and re-layouts: 27.7 us -> 1.25 us
  between operations: 14.2 us -> 1.35 us
  matrix products: 12.5 us -> 0 us
  loops' own time: 0 us -> 7.45 us
  other arithmetic: 6.33 us -> 0 us
    reduce_scatter x1 -> x0, waiting for transfers between devices: 222 us -> none  [per_device(): lax.psum_scatter(partial_value.astype(jnp.bfloat16), 'tp', scatter_dimens...]
    pallas_call x0 -> x2, Pallas kernels: none -> 122 us  [the longest x1 105 us: experts_call(): pl.pallas_call(functools.partial(expert_kernel, nep, nt, width, size, pie...]
    all_to_all x2 -> x0, blocking collectives: 115 us -> none  [the longest x1 100 us: per_device(): lax.all_to_all(outgoing, 'ep', split_axis=0, concat_axis=0, tiled=True)]
    all_gather x1 -> x0, waiting for transfers between devices: 82.9 us -> none  [per_device(): portion = lax.all_gather(returned, 'tp', axis=2, tiled=True)]
    all_gather x1 -> x0, blocking collectives: 55.7 us -> none  [per_device(): projected = lax.all_gather(columns, 'tp', axis=1, tiled=True)]
    dot_general x3 -> x0, matrix products: 12.5 us -> none  [the longest x1 8.77 us: expert_terms(): jnp.einsum('scmf,cfd->scmd', hidden, down_weight, preferred_element_type=...]
    another operation x0 -> x1, loops' own time: none -> 7.45 us  [per_device(): return lax.switch(choice[0], branches, *operands)]
    gather x2 -> x0, local copies, waits for them, and re-layouts: 7.43 us -> none  [the longest x1 6.02 us: per_device(): outgoing = jnp.take(normed, rows_table, axis=0)]
  transfers between devices with their start and end apart: 2 -> 0, of which waited for: 2 -> 0; matrix products, arithmetic and copies ran while one was open for 0% -> 0% of each run, Pallas kernels for 0% -> 0%
where the time goes in v2:
time: 132 us
  Pallas kernels  122 us (92%)
  loops' own time  7.45 us (6%)
  between operations  1.35 us (1%)
    pallas_call x1, Pallas kernels, experts_call(): pl.pallas_call(functools.partial(expert_kernel, nep, nt, width, size, pie...  105 us
    pallas_call x1, Pallas kernels, collect(): pl.pallas_call(functools.partial(collect_kernel, nep, nt, sizes), out_sha...  17.4 us
    another operation x1, loops' own time, per_device(): return lax.switch(choice[0], branches, *operands)  7.45 us

profile of v2, /device:TPU:8, one launch (start us, length us, event | category | flops | bytes accessed | tf_op | source)
XLA Modules:
  0.0 132.0 jit_solution(12359861052214924386)
XLA Ops:
  0.6 0.0 copy-start
  0.6 0.0 copy-start.2
  0.7 0.0 copy-start.3
  0.7 17.4 %collect.1 = (bf16[8,64,128]{2,1,0:T(8,128)(2,1)S(1)}, bf16[2,8,16,128]{3,2,1,0:T(8,128)(2,1)S(1)}, f32[2,2,8,128]{3,2,1,0:T(8,128)S(1)}, s32[1]{0:T(128)}) custom-call(bf16[128,2048]{1,0:T(8,128)(2,1)} %attn.1, bf16[64,2048]{1,0:T(8,128)(2,1)} %bitcast.19, bf16[128,2048]{1,0:T(8,128)(2,1)} %residual.1, s32[2,128]{1,0:T(2,128)} %bitcast.30, s32[8,16]{1,0:T(8,128)} %bitcast.29), custom_call_target="tpu_custom_call" | custom-call | tf_op jit(solution)/shard_map/collect/pallas_call | solution.py:575
  18.0 0.0 copy-start.1
  18.7 0.0 copy-done
  18.7 0.0 copy-done.2
  18.7 0.0 copy-done.3
  18.7 0.0 copy-done.1
  18.7 112.0 %conditional.1 = ((bf16[4,2048]{1,0:T(4,128)(2,1)S(1)}, bf16[4,2048]{1,0:T(4,128)(2,1)S(1)})) conditional(s32[]{:T(128)} %bitcast.9, (bf16[8,64,128]{2,1,0:T(8,128)(2,1)S(1)}, bf16[2,8,16,128]{3,2,1,0:T(8,128)(2,1)S(1)}, f32[2,2,8,128]{3,2,1,0:T(8,128)S(1)}, f32[8,128]{1,0:T(8,128)S(1)}, f32[2048]{0:T(1024)S(1)}, ...), branch_computations={%region_0.0_spmd, %region_1.0_spmd, %region_2.0_spmd} | conditional | bytes 8 | solution.py:663
  26.0 104.6 %experts_1024.1 = (bf16[4,2048]{1,0:T(4,128)(2,1)S(1)}, bf16[4,2048]{1,0:T(4,128)(2,1)S(1)}) custom-call(bf16[8,64,128]{2,1,0:T(8,128)(2,1)S(1)} %get-tuple-element.72.rows, bf16[2,8,16,128]{3,2,1,0:T(8,128)(2,1)S(1)} %get-tuple-element.73.names, f32[2,2,8,128]{3,2,1,0:T(8,128)S(1)} %get-tuple-element.74.aims, f32[8,128]{1,0:T(8,128)S(1)} %get-tuple-element.75.logits, ...), custom_call_target="tpu_custom_call" | custom-call | tf_op jit(solution)/shard_map/cond/branch_2_fun/experts_1024/pallas_call | solution.py:609
  130.8 0.6 copy.36
  131.4 0.6 copy.37
Async XLA Ops:
  0.6 18.1 %copy-start = (bf16[1,2048,176]{1,2,0:T(8,128)(2,1)S(1)}, bf16[1,2048,176]{1,2,0:T(8,128)(2,1)}, u32[]{:S(2)}) copy-start(bf16[1,2048,176]{1,2,0:T(8,128)(2,1)} %param.21) | copy-start | bytes 2162692
  0.6 18.1 %copy-start.2 = (f32[2048]{0:T(1024)S(1)}, f32[2048]{0:T(1024)}, u32[]{:S(2)}) copy-start(f32[2048]{0:T(1024)} %param.24) | copy-start | bytes 24580
  0.7 18.1 %copy-start.3 = (f32[128,8]{0,1:T(8,128)S(1)}, f32[128,8]{0,1:T(8,128)}, u32[]{:S(2)}) copy-start(f32[128,8]{0,1:T(8,128)} %param.18) | copy-start | bytes 12292
  18.0 0.7 copy-start.1

commit v3 on v2

--- a/solution.py
+++ b/solution.py
@@ -18,90 +18,87 @@
 SIGNS = (1, -1)
 
 
-def row_range(parts, part, sign, dist, count):
-    start, size = parts[part]
+def row_range(rows, sign, dist, count):
     if 2 * dist == count:
-        half = size // 2
-        return (start, half) if sign > 0 else (start + half, half)
-    return (start, size)
-
-
-def split_rows(half, pieces):
-    units, out, at, taken = half // 32, [], 0, 0
-    for i in range(pieces):
-        size = (units * (i + 1) // pieces) * 32 - at
-        first = int(0.41 * (at + size) / 32 + 0.5) * 32 - taken
-        first = min(max(first, 32), size - 32)
-        out.append((at, first, size - first))
-        at, taken = at + size, taken + first
-    return out
-
-
-def part_of(pieces, u):
-    start, first, second = pieces[u]
-    return {"a": (start, first), "b": (start + first, second)}
-
-
-def gather_sends(nz, nx, pieces, u):
-    count, parts, sends = {"z": nz, "x": nx}, part_of(pieces, u), {}
-    for part, (first, second) in (("a", ("x", "z")), ("b", ("z", "x"))):
-        for axis in (first, second):
-            n = count[axis]
-            for other in range(1 if axis == first else count[first]):
-                for dist in range(1, n // 2 + 1):
-                    for sign in SIGNS:
-                        need = set()
-                        if dist > 1:
-                            need.add(("g", u, part, axis, sign, dist - 1, other))
-                        elif axis == second and other:
-                            m = count[first]
-                            if 2 * other <= m:
-                                need.add(("g", u, part, first, 1, other, 0))
-                            if 2 * other >= m:
-                                need.add(("g", u, part, first, -1, m - other, 0))
-                        size = row_range(parts, part, sign, dist, n)[1]
-                        sends[("g", u, part, axis, sign, dist, other)] = ((axis, sign), size, need)
+        half = rows // 2
+        return (0, half) if sign > 0 else (half, half)
+    return (0, rows)
+
+
+AXES = (("z", "x"), ("x", "z"))
+NEXT = {1: 0, 2: 1, 3: 2, 4: 3}
+PAIR = {1: 0, 2: 0, 3: 2, 4: 2}
+
+
+def ring_of(axis, core, n, rows):
+    if axis == "z":
+        ring = PAIR if core == 0 and rows <= 256 else NEXT
+    else:
+        ring = PAIR if rows <= 320 else NEXT
+    return {d: p for d, p in ring.items() if 2 * d <= n}
+
+
+def steps_of(nz, nx, rows):
+    found = set()
+    for core in range(2):
+        for axis, n in (("z", nz), ("x", nx)):
+            for dist, near in ring_of(axis, core, n, rows).items():
+                for sign in SIGNS:
+                    found.add((axis, sign * (dist - near) % n))
+    return sorted(found)
+
+
+def gather_sends(nz, nx, rows, core):
+    count, sends = {"z": nz, "x": nx}, {}
+    first, second = AXES[core]
+    for axis in (first, second):
+        n = count[axis]
+        ring = ring_of(axis, core, n, rows)
+        for other in range(1 if axis == first else count[first]):
+            for dist, near in ring.items():
+                for sign in SIGNS:
+                    need = set()
+                    if near:
+                        need.add(("g", axis, sign, near, other))
+                    elif axis == second and other:
+                        m = count[first]
+                        if 2 * other <= m:
+                            need.add(("g", first, 1, other, 0))
+                        if 2 * other >= m:
+                            need.add(("g", first, -1, m - other, 0))
+                    size = row_range(rows, sign, dist, n)[1]
+                    sends[("g", axis, sign, dist, other)] = ((axis, sign), size * (dist - near), need)
     return sends
 
 
-def reduce_sends(nz, nx, pieces, u):
-    count, parts, sends = {"z": nz, "x": nx}, part_of(pieces, u), {}
-    for part, (first, second) in (("a", ("z", "x")), ("b", ("x", "z"))):
-        for axis in (first, second):
-            n = count[axis]
-            for other in range(count[second] if axis == first else 1):
-                for dist in range(n // 2, 0, -1):
-                    for sign in SIGNS:
-                        offset = (sign * dist) % n
-                        need = {("c", u, offset if axis == "z" else other)}
-                        if 2 * dist < n:
-                            need.add(("r", u, part, axis, sign, dist + 1, other))
-                        if axis == second:
-                            for way in SIGNS:
-                                need.add(("r", u, part, first, way, 1, offset))
-                        size = row_range(parts, part, sign, dist, n)[1]
-                        sends[("r", u, part, axis, sign, dist, other)] = ((axis, sign), size, need)
+def reduce_sends(nz, nx, rows, core):
+    count, sends = {"z": nz, "x": nx}, {}
+    second, first = AXES[core]
+    for axis in (first, second):
+        n = count[axis]
+        ring = ring_of(axis, core, n, rows)
+        for other in range(count[second] if axis == first else 1):
+            for dist in sorted(ring, reverse=True):
+                for sign in SIGNS:
+                    offset = (sign * dist) % n
+                    need = {("c", offset if axis == "z" else other)}
+                    for further, near in ring.items():
+                        if near == dist:
+                            need.add(("r", axis, sign, further, other))
+                    if axis == second:
+                        for further, near in ring_of(first, core, count[first], rows).items():
+                            if near == 0:
+                                for way in SIGNS:
+                                    need.add(("r", first, way, further, offset))
+                    size = row_range(rows, sign, dist, n)[1]
+                    sends[("r", axis, sign, dist, other)] = (
+                        (axis, sign), size * (dist - ring[dist]), need
+                    )
     return sends
 
 
-def schedule(nz, nx, pieces):
-    rate, latency = 181.0, 1.7
-    sends, tasks, landing, total = {}, {}, {}, 0
-    far = sorted(range(nz), key=lambda d: (-min(d, nz - d), d))
-    for u, (_, first, second) in enumerate(pieces):
-        gathers = gather_sends(nz, nx, pieces, u)
-        reduces = reduce_sends(nz, nx, pieces, u)
-        sends.update(gathers)
-        sends.update(reduces)
-        rows = first + second
-        tasks[("x", u)] = (rows * 0.011, set(gathers))
-        before = ("x", u)
-        for dz in far:
-            tasks[("c", u, dz)] = (rows * 0.0007, {before})
-            before = ("c", u, dz)
-        for key, value in reduces.items():
-            landing[key] = (total, value[1])
-            total += value[1]
+def timeline(sends, tasks):
+    rate, latency = 330.0, 1.7
     done, free, ops, arrivals = set(), {}, [], []
     waiting, later, now = dict(sends), dict(tasks), 0.0
 
@@ -130,7 +127,26 @@
             continue
         now = max(now, arrivals[0][0])
     assert not waiting
-    return {key: i for i, key in enumerate(sends)}, ops, landing, total
+    return ops
+
+
+def gather_plan(nz, nx, rows, core):
+    sends = gather_sends(nz, nx, rows, core)
+    return list(sends), timeline(sends, {})
+
+
+def reduce_plan(nz, nx, rows, core):
+    sends = reduce_sends(nz, nx, rows, core)
+    tasks, before = {}, set()
+    for dz in sorted(range(nz), key=lambda d: (-min(d, nz - d), d)):
+        tasks[("c", dz)] = (rows * 0.0009, before)
+        before = {("c", dz)}
+    landing, total = {}, 0
+    for key, value in sends.items():
+        many = row_range(rows, key[2], key[3], nz if key[1] == "z" else nx)[1]
+        landing[key] = (total, many)
+        total += many
+    return list(sends), timeline(sends, tasks), landing, total
 
 
 def iota(shape, dim):
@@ -252,12 +268,12 @@
 
 
 def expert_kernel(
-    nep, nt, width, size, count_pieces,
+    nep, nt, width, size,
     rows, names, aims, logits, gain_in, gain_out, w_gate, w_up, w_down,
     layer_out, next_out,
     pick, flat_l, flat_r, spots, got, full, gates, ups, downs, hid, share, landed, ret_pick, ret_start,
     ret_l, ret_r, back, slots, outgoing, incoming, whole,
-    t_send, t_recv, w_local, w_send, w_recv, e_send, e_recv, f_send, f_recv,
+    g_send, g_recv, r_send, r_recv, w_local, w_send, w_recv, e_send, e_recv, f_send, f_recv,
 ):
     ep, tp = lax.axis_index("ep"), lax.axis_index("tp")
     nx = NX if nt > 8 else 2
@@ -267,7 +283,6 @@
     mate = 2 * y + (1 - core)
     z, x = tp // nx, lax.rem(tp, nx)
     hp = size // 2
-    pieces = split_rows(hp, count_pieces)
     own_rows = GROUP // nt
     count = {"z": nz, "x": nx}
 
@@ -280,7 +295,7 @@
         return {"ep": 2 * lax.rem(y + k, ny) + core, "tp": tp}
 
     partner = {"ep": mate, "tp": tp}
-    friends = [neighbour(axis, sign) for axis in ("z", "x") for sign in SIGNS] + [partner]
+    friends = [neighbour(axis, step) for axis, step in steps_of(nz, nx, hp)] + [partner]
     friends += [plane_peer(k) for k in range(1, ny)]
     barrier = pltpu.get_barrier_semaphore()
     for friend in friends:
@@ -357,62 +372,66 @@
     def slot_of(axis, offset, other):
         return (offset % nz, other) if axis == "z" else (other, offset % nx)
 
-    index, ops, landing, _ = schedule(nz, nx, pieces)
-
-    def transfer(key):
-        kind, u, part, axis, sign, dist, other = key
-        start, many = row_range(part_of(pieces, u), part, sign, dist, count[axis])
-        i = index[key]
-        if kind == "g":
-            src, dst = slot_of(axis, sign * (dist - 1), other), slot_of(axis, sign * dist, other)
-            target = got.at[dst[0], dst[1], pl.ds(start, many), :]
-            source = got.at[src[0], src[1], pl.ds(start, many), :]
-        else:
-            src = slot_of(axis, sign * dist, other)
-            target = landed.at[pl.ds(landing[key][0], many), :]
-            source = share.at[src[0], src[1], pl.ds(start, many), :]
-        return move(source, target, t_send.at[i], t_recv.at[i], neighbour(axis, sign))
-
-    def add_landed(key):
-        _, u, part, axis, sign, dist, other = key
-        start, many = row_range(part_of(pieces, u), part, sign, dist, count[axis])
-        at = slot_of(axis, sign * (dist - 1), other)
-        here, there = pl.ds(start, many), pl.ds(landing[key][0], many)
+    gathers = [gather_plan(nz, nx, hp, c) for c in range(2)]
+    reduces = [reduce_plan(nz, nx, hp, c) for c in range(2)]
+
+    def gather_copy(c, key):
+        _, axis, sign, dist, other = key
+        start, many = row_range(hp, sign, dist, count[axis])
+        near = ring_of(axis, c, count[axis], hp)[dist]
+        src, dst = slot_of(axis, sign * near, other), slot_of(axis, sign * dist, other)
+        i = gathers[c][0].index(key)
+        return move(
+            got.at[src[0], src[1], pl.ds(start, many), :],
+            got.at[dst[0], dst[1], pl.ds(start, many), :],
+            g_send.at[i], g_recv.at[i], neighbour(axis, sign * (dist - near)),
+        )
+
+    def reduce_copy(c, key):
+        _, axis, sign, dist, other = key
+        start, many = row_range(hp, sign, dist, count[axis])
+        near = ring_of(axis, c, count[axis], hp)[dist]
+        src = slot_of(axis, sign * dist, other)
+        i = reduces[c][0].index(key)
+        return move(
+            share.at[src[0], src[1], pl.ds(start, many), :],
+            landed.at[pl.ds(reduces[c][2][key][0], many), :],
+            r_send.at[i], r_recv.at[i], neighbour(axis, sign * (dist - near)),
+        )
+
+    def add_landed(c, key):
+        _, axis, sign, dist, other = key
+        start, many = row_range(hp, sign, dist, count[axis])
+        at = slot_of(axis, sign * ring_of(axis, c, count[axis], hp)[dist], other)
+        here, there = pl.ds(start, many), pl.ds(reduces[c][2][key][0], many)
         share[at[0], at[1], here, :] = (
             share[at[0], at[1], here, :].astype(F32) + landed[there, :].astype(F32)
         ).astype(BF16)
 
     core_f = core.astype(F32)
 
-    def experts(u):
-        start, many = pieces[u][0], pieces[u][1] + pieces[u][2]
-        at = 2 * start
-        here = pl.ds(start, many)
-        left = left_half((many, 128))
-
+    left = left_half((hp, 128))
+
+    def experts():
         def join(i, carry):
             p0, p1 = [
-                got[
-                    lax.rem(z - t // nx + nz, nz), lax.rem(x - lax.rem(t, nx) + nx, nx), here, :
-                ].astype(F32)
+                got[lax.rem(z - t // nx + nz, nz), lax.rem(x - lax.rem(t, nx) + nx, nx)].astype(F32)
                 for t in (2 * i, 2 * i + 1)
             ]
             lanes = pl.ds(pl.multiple_of(i * 128, 128), 128)
-            full[at : at + many, lanes] = jnp.where(left, p0, swap(p1)).astype(BF16)
-            full[at + many : at + 2 * many, lanes] = jnp.where(left, swap(p0), p1).astype(BF16)
+            full[0:hp, lanes] = jnp.where(left, p0, swap(p1)).astype(BF16)
+            full[hp:size, lanes] = jnp.where(left, swap(p0), p1).astype(BF16)
             return carry
 
         lax.fori_loop(0, nt // 2, join, 0)
-        tile = next(t for t in (128, 96, 160, 64, 32) if many % t == 0)
-        sides = many // tile
+        tile = next(t for t in (128, 192, 64) if size % t == 0)
 
         def one(i, carry):
-            span = pl.ds(pl.multiple_of(at + i * tile, 32), tile)
+            span = pl.ds(pl.multiple_of(i * tile, tile), tile)
             value = full[span, :].astype(F32)
             scale = lax.rsqrt(jnp.sum(value * value, axis=1, keepdims=True) * (1.0 / width) + 1e-06)
             normed = (value * scale * gain_in[...]).astype(BF16)
-            first = start + lax.rem(i, sides) * tile + (i // sides) * hp
-            spot = (iota((tile, 1), 0) + first).astype(F32)
+            spot = (iota((tile, 1), 0) + i * tile).astype(F32)
             in_low = (spot < jnp.broadcast_to(count_low, (tile, 1))).astype(F32)
             mine = in_low * (1.0 - core_f) + (1.0 - in_low) * core_f
             for w, keep in ((0, mine), (1, 1.0 - mine)):
@@ -422,55 +441,37 @@
                 hid[w, span, :] = jnp.where(keep > 0.5, value_h, 0.0).astype(BF16)
             return carry
 
-        lax.fori_loop(0, 2 * sides, one, 0)
-
-    def down(u, dz):
-        start, many = pieces[u][0], pieces[u][1] + pieces[u][2]
-        left = left_half((many, 128))
+        lax.fori_loop(0, size // tile, one, 0)
+
+    def down(dz):
         lanes = pl.ds(pl.multiple_of(lax.rem(z + dz, nz) * (nx * COLS), 128), nx * COLS)
         wd = [downs[w, :, lanes] for w in range(2)]
         sides = []
         for q in range(2):
-            at = slice(2 * start + q * many, 2 * start + (q + 1) * many)
+            at = slice(q * hp, (q + 1) * hp)
             sides.append(
                 jnp.dot(hid[0, at, :], wd[0], preferred_element_type=F32)
                 + jnp.dot(hid[1, at, :], wd[1], preferred_element_type=F32)
             )
-        here = pl.ds(start, many)
         for i in range(nx // 2):
             top, bottom = [v[:, i * 128 : (i + 1) * 128] for v in sides]
             d0 = lax.rem(2 * i - x + nx, nx)
             d1 = lax.rem(2 * i + 1 - x + nx, nx)
-            share[dz, d0, here, :] = jnp.where(left, top, swap(bottom)).astype(BF16)
-            share[dz, d1, here, :] = jnp.where(left, swap(top), bottom).astype(BF16)
-
-    sent = list(mate_weights)
+            share[dz, d0] = jnp.where(left, top, swap(bottom)).astype(BF16)
+            share[dz, d1] = jnp.where(left, swap(top), bottom).astype(BF16)
+
     for c in mate_weights:
         c.start()
-    have_weights = False
-    for kind, key in ops:
-        if kind == "task":
-            if key[0] == "x":
-                if not have_weights:
-                    have_weights = True
-                    for c in own_weights:
-                        c.wait()
-                    for c in mate_weights:
-                        c.wait_recv()
-                experts(key[1])
-            else:
-                down(key[1], key[2])
-            continue
-        c = transfer(key)
-        if kind == "start":
-            c.start()
-            sent.append(c)
-        else:
-            c.wait_recv()
-            if key[0] == "r":
-                add_landed(key)
-
-    left = left_half((hp, 128))
+
+    for c in range(2):
+
+        @pl.when(core == c)
+        def _(c=c):
+            for kind, key in gathers[c][1]:
+                if kind == "wait":
+                    break
+                gather_copy(c, key).start()
+
     half_cap = CAP // 2
     lead = (iota((half_cap, size), 1) - iota((half_cap, size), 0)).astype(F32)
     for q in range(2):
@@ -483,6 +484,47 @@
                 return carry
 
             lax.fori_loop(0, ny, mark, 0)
+
+    for c in range(2):
+
+        @pl.when(core == c)
+        def _(c=c):
+            begun = False
+            for kind, key in gathers[c][1]:
+                begun = begun or kind == "wait"
+                if kind == "wait":
+                    gather_copy(c, key).wait_recv()
+                elif begun:
+                    gather_copy(c, key).start()
+
+    for c in own_weights:
+        c.wait()
+    for c in mate_weights:
+        c.wait_recv()
+    experts()
+
+    runs = []
+    for c in range(2):
+        runs.append([])
+        for kind, key in reduces[c][1]:
+            if kind == "task":
+                runs[c].append((key[1], []))
+            else:
+                runs[c][-1][1].append((kind, key))
+    for stage in range(nz):
+        assert runs[0][stage][0] == runs[1][stage][0]
+        down(runs[0][stage][0])
+        for c in range(2):
+
+            @pl.when(core == c)
+            def _(c=c, stage=stage):
+                for kind, key in runs[c][stage][1]:
+                    if kind == "start":
+                        reduce_copy(c, key).start()
+                    else:
+                        reduce_copy(c, key).wait_recv()
+                        add_landed(c, key)
+
     v = share[0, 0].astype(F32)
     w = swap(v)
     ret_l[0:hp, :] = jnp.where(left, v, 0.0).astype(BF16)
@@ -502,8 +544,18 @@
     ]
     for c in returns:
         c.start()
-        sent.append(c)
     slots[y] = back[y]
+    for c in mate_weights:
+        c.wait_send()
+    for c in range(2):
+
+        @pl.when(core == c)
+        def _(c=c):
+            for key in gathers[c][0]:
+                gather_copy(c, key).wait_send()
+            for key in reduces[c][0]:
+                reduce_copy(c, key).wait_send()
+
 
     own_ids = names[core, y].astype(F32)
     experts_all = logits.shape[0]
@@ -552,8 +604,9 @@
     ]
     for c in owners:
         c.start()
-        sent.append(c)
     incoming[tp] = outgoing[tp]
+    for c in returns + owners:
+        c.wait_send()
     for k in range(1, nt):
         owner_copy(k, tp, lax.rem(tp + nt - k, nt)).wait_recv()
     left_own = left_half((own_rows, 128))
@@ -564,8 +617,6 @@
     layer_out[...] = value.astype(BF16)
     scale = lax.rsqrt(jnp.sum(value * value, axis=1, keepdims=True) * (1.0 / width) + 1e-06)
     next_out[...] = (value * scale * gain_out[...]).astype(BF16)
-    for c in sent:
-        c.wait_send()
 
 
 def collect(attn_out, w_out, residual_in, ids, copies, nep, nt, sizes):
@@ -594,7 +645,7 @@
     )(attn_out, w_out, residual_in, ids, copies)
 
 
-def experts_call(size, which, pieces, nep, nt, rows, names, aims, logits, gain_in, gain_out, w_gate, w_up, w_down):
+def experts_call(size, which, nep, nt, rows, names, aims, logits, gain_in, gain_out, w_gate, w_up, w_down):
     vmem = pl.BlockSpec(memory_space=pltpu.VMEM)
     hbm = pl.BlockSpec(memory_space=pl.ANY)
     inner, width = w_gate.shape[1], w_gate.shape[2]
@@ -603,11 +654,12 @@
     ny = nep // 2
     hp = size // 2
     own_rows = GROUP // nt
-    index, _, _, land = schedule(nz, nx, split_rows(hp, pieces))
+    many = len(gather_plan(nz, nx, hp, 0)[0]), len(gather_plan(nz, nx, hp, 1)[0])
+    land = max(reduce_plan(nz, nx, hp, c)[3] for c in range(2))
     dma = pltpu.SemaphoreType.DMA
     out = jax.ShapeDtypeStruct((own_rows, width), BF16)
     return pl.pallas_call(
-        functools.partial(expert_kernel, nep, nt, width, size, pieces),
+        functools.partial(expert_kernel, nep, nt, width, size),
         out_shape=(out, out),
         in_specs=[vmem] * 6 + [hbm] * 3,
         out_specs=(vmem, vmem),
@@ -633,7 +685,8 @@
             pltpu.VMEM((nt, own_rows, 128), BF16),
             pltpu.VMEM((nt, own_rows, 128), BF16),
             pltpu.VMEM((own_rows, width), F32),
-            dma((len(index),)), dma((len(index),)),
+            dma((max(many),)), dma((max(many),)),
+            dma((max(many),)), dma((max(many),)),
             dma((3,)), dma((3,)), dma((3,)),
             dma((ny,)), dma((ny,)),
             dma((nt,)), dma((nt,)),
@@ -648,22 +701,21 @@
 def per_device(sizes, attn_out, residual_in, w_out, gain_in, router_logits, expert_ids, copy_of, w_gate, w_up, w_down, gain_out):
     nt, nep = lax.axis_size("tp"), lax.axis_size("ep")
     rows, names, aims, choice = collect(
-        attn_out, w_out.T, residual_in, expert_ids.T, copy_of.T, nep, nt, tuple(s for s, _ in sizes)
+        attn_out, w_out.T, residual_in, expert_ids.T, copy_of.T, nep, nt, sizes
     )
     operands = (
         rows, names, aims, router_logits.T, gain_in[None, :], gain_out[None, :],
         jnp.swapaxes(w_gate, 1, 2), jnp.swapaxes(w_up, 1, 2), w_down,
     )
     branches = [
-        functools.partial(experts_call, size, i + 1, pieces, nep, nt)
-        for i, (size, pieces) in enumerate(sizes)
+        functools.partial(experts_call, size, i + 1, nep, nt) for i, size in enumerate(sizes)
     ]
     if len(branches) == 1:
         return branches[0](*operands)
     return lax.switch(choice[0], branches, *operands)
 
 
-def solution(mesh, sizes=((512, 1), (640, 1), (1024, 1))):
+def solution(mesh, sizes=(512, 640, 768, 1024)):
     return jax.shard_map(
         functools.partial(per_device, sizes),
         mesh=mesh,

time: 132 us -> 89.4 us (0.68)
  Pallas kernels: 122 us -> 86 us
  loops' own time: 7.45 us -> 0.55 us
    pallas_call x1, Pallas kernels: 105 us -> 68.6 us  [experts_call(): pl.pallas_call(functools.partial(expert_kernel, nep, nt, width, size), ou...]
    another operation x1, loops' own time: 7.45 us -> 0.55 us  [per_device(): return lax.switch(choice[0], branches, *operands)]
where the time goes in v3:
time: 89.4 us; the launch traced here: 89.1 us
  Pallas kernels  86 us (96%)
  between operations  1.35 us (2%)
  local copies, waits for them, and re-layouts  1.24 us (1%)
    pallas_call x1, Pallas kernels, experts_call(): pl.pallas_call(functools.partial(expert_kernel, nep, nt, width, size), ou...  68.6 us
    pallas_call x1, Pallas kernels, collect(): pl.pallas_call(functools.partial(collect_kernel, nep, nt, sizes), out_sha...  17.4 us

profile of v3, /device:TPU:8, one launch (start us, length us, event | category | flops | bytes accessed | tf_op | source)
XLA Modules:
  0.0 89.1 jit_solution(4324977505473780951)
XLA Ops:
  0.6 0.0 copy-start
  0.6 0.0 copy-start.2
  0.7 0.0 copy-start.3
  0.7 17.4 %collect.1 = (bf16[8,64,128]{2,1,0:T(8,128)(2,1)S(1)}, bf16[2,8,16,128]{3,2,1,0:T(8,128)(2,1)S(1)}, f32[2,2,8,128]{3,2,1,0:T(8,128)S(1)}, s32[1]{0:T(128)}) custom-call(bf16[128,2048]{1,0:T(8,128)(2,1)} %attn.1, bf16[64,2048]{1,0:T(8,128)(2,1)} %bitcast.23, bf16[128,2048]{1,0:T(8,128)(2,1)} %residual.1, s32[2,128]{1,0:T(2,128)} %bitcast.37, s32[8,16]{1,0:T(8,128)} %bitcast.36), custom_call_target="tpu_custom_call" | custom-call | tf_op jit(solution)/shard_map/collect/pallas_call | solution.py:626
  18.0 0.0 copy-start.1
  18.7 0.0 copy-done
  18.7 0.0 copy-done.2
  18.7 0.0 copy-done.3
  18.7 0.0 copy-done.1
  18.7 69.2 %conditional.1 = ((bf16[4,2048]{1,0:T(4,128)(2,1)S(1)}, bf16[4,2048]{1,0:T(4,128)(2,1)S(1)})) conditional(s32[]{:T(128)} %bitcast.11, (bf16[8,64,128]{2,1,0:T(8,128)(2,1)S(1)}, bf16[2,8,16,128]{3,2,1,0:T(8,128)(2,1)S(1)}, f32[2,2,8,128]{3,2,1,0:T(8,128)S(1)}, f32[8,128]{1,0:T(8,128)S(1)}, f32[2048]{0:T(1024)S(1)}, ...), branch_computations={%region_0.0_spmd, %region_1.0_spmd, %region_2.0_spmd, %region_3.0_... | conditional | bytes 8 | solution.py:715
  18.7 68.6 %experts_512.1 = (bf16[4,2048]{1,0:T(4,128)(2,1)S(1)}, bf16[4,2048]{1,0:T(4,128)(2,1)S(1)}) custom-call(bf16[8,64,128]{2,1,0:T(8,128)(2,1)S(1)} %get-tuple-element.72.rows, bf16[2,8,16,128]{3,2,1,0:T(8,128)(2,1)S(1)} %get-tuple-element.73.names, f32[2,2,8,128]{3,2,1,0:T(8,128)S(1)} %get-tuple-element.74.aims, f32[8,128]{1,0:T(8,128)S(1)} %get-tuple-element.75.logits, ...), custom_call_target="tpu_custom_call" | custom-call | tf_op jit(solution)/shard_map/cond/branch_0_fun/experts_512/pallas_call | solution.py:661
  87.9 0.6 copy.43
  88.5 0.6 copy.44
Async XLA Ops:
  0.6 18.1 %copy-start = (bf16[1,2048,176]{1,2,0:T(8,128)(2,1)S(1)}, bf16[1,2048,176]{1,2,0:T(8,128)(2,1)}, u32[]{:S(2)}) copy-start(bf16[1,2048,176]{1,2,0:T(8,128)(2,1)} %param.22) | copy-start | bytes 2162692
  0.6 18.1 %copy-start.2 = (f32[2048]{0:T(1024)S(1)}, f32[2048]{0:T(1024)}, u32[]{:S(2)}) copy-start(f32[2048]{0:T(1024)} %param.25) | copy-start | bytes 24580
  0.7 18.1 %copy-start.3 = (f32[128,8]{0,1:T(8,128)S(1)}, f32[128,8]{0,1:T(8,128)}, u32[]{:S(2)}) copy-start(f32[128,8]{0,1:T(8,128)} %param.19) | copy-start | bytes 12292
  18.0 0.7 copy-start.1
